TPU v7x, 32 devices: a whole 2x2x4 slice. The times are simulated.
32 devices in a mesh: member: 4 (over z), space: 8 (over y, x, core).
Axes of the slice: x: 2, y: 2, z: 4, core: 2. Of those that a mesh axis runs over, the one named last changes fastest.
Arguments:
- particles: float32 [32, 2, 200, 800], P('member', None, 'space'), may hold values from -8 to 8
- loglik_grad: float32 [32, 2, 200, 800], P('member', None, 'space'), may hold values from -0.00036621094 to 0.00036621094
- wave_prev: float32 [32, 2, 200, 800], P('member', None, 'space'), may hold values from -6 to 6
- wave_now: float32 [32, 2, 200, 800], P('member', None, 'space'), may hold values from -6 to 6
- ghosts: float32 [32, 8, 200, 800], P('member', None, 'space'), may hold values from -6 to 6
- src_cell: int32 [32], P('member'), may hold values from 0 to 159999
Outputs:
- new_particles: float32 [32, 2, 200, 800], P('member', None, 'space')
- wave_before: float32 [32, 2, 200, 800], P('member', None, 'space')
- wave_after: float32 [32, 2, 200, 800], P('member', None, 'space')
Inputs may be any that keep to these rules, and one draw needn't show every extreme that they name: `src_cell`: the flat index 800 * x + y of each particle's source cell on depth plane 0.
All inputs are finite; a program needn't handle non-finite values.
Results may differ from a plain program's by a relative error of at most 0.0003.
Values sent between devices are 32-bit elements; how exact they have to be, the bound alone decides.
No kernel may reach another device: no remote copies, remote signals or barrier semaphores. Data moves between devices by JAX's collectives and lax.ppermute only.
A program may use at most 128 MiB of HBM per device.

v0:
```python
import functools
import math

import jax
import jax.numpy as jnp
from jax import lax
from jax.experimental import pallas as pl
from jax.experimental.pallas import tpu as pltpu
from jax.sharding import PartitionSpec as P


GHOST = 4
STEPS = 4
LANES = 128

weights = (-205.0 / 72.0, 8.0 / 5.0, -1.0 / 5.0, 8.0 / 315.0, -1.0 / 560.0)
step_size = 0.25
courant = 0.3

VMEM = pl.BlockSpec(memory_space=pltpu.VMEM)
SMEM = pl.BlockSpec(memory_space=pltpu.SMEM)


ANY = pl.BlockSpec(memory_space=pl.ANY)


def held(shape, space=pltpu.VMEM):
    return space(tuple(shape), jnp.float32)


def call(body, out_shape, in_specs, out_specs, operands, scratch_shapes=(), after=()):
    count = len(operands)

    def ordered(*refs):
        body(*refs[:count], *refs[count + len(after) :])

    return pl.pallas_call(
        ordered,
        out_shape=out_shape,
        in_specs=in_specs + [ANY] * len(after),
        out_specs=out_specs,
        scratch_shapes=scratch_shapes,
        compiler_params=pltpu.CompilerParams(vmem_limit_bytes=24 << 20),
    )(*operands, *after)


class Packing:
    def __init__(self, width, depth, across, members):
        self.width, self.depth, self.across, self.members = width, depth, across, members
        self.rows = width * depth
        self.full = across // LANES
        self.tail = across % LANES
        self.group = LANES // self.tail if self.tail else 1
        self.tail_tiles = -(-self.rows // self.group) if self.tail else 0
        total = self.rows * self.full + self.tail_tiles
        self.tiles = -(-total // members)
        self.lanes = self.tiles * LANES
        self.spare = self.tiles * members - total

    def runs(self, row):
        tile, at, left = row * self.full, 0, self.full
        while left:
            chunk, place = divmod(tile, self.tiles)
            count = min(left, self.tiles - place)
            yield chunk, place * LANES, at * LANES, count * LANES
            tile, at, left = tile + count, at + count, left - count

    def tail_place(self, index):
        chunk, place = divmod(self.rows * self.full + index, self.tiles)
        return chunk, place * LANES


def pack_body(pack, cuts, me_ref, cells_ref, *refs):
    outs, buf = refs[:-1], refs[-1]
    own = cells_ref.shape[2]
    me = me_ref[0]
    slots = [lax.rem(chunk - me + pack.members, pack.members) for chunk in range(pack.members)]
    for row in range(pack.rows):
        x, z = divmod(row, pack.depth)
        for chunk, there, here, count in pack.runs(row):
            buf[slots[chunk], :, there : there + count] = cells_ref[x, z, :, here : here + count]
    start = pack.full * LANES
    for index in range(pack.tail_tiles):
        chunk, place = pack.tail_place(index)
        pieces = []
        for row in range(index * pack.group, min(pack.rows, (index + 1) * pack.group)):
            x, z = divmod(row, pack.depth)
            pieces.append(cells_ref[x, z, :, start : start + pack.tail])
        empty = LANES - pack.tail * len(pieces)
        if empty:
            pieces.append(jnp.zeros((own, empty), jnp.float32))
        buf[slots[chunk], :, place : place + LANES] = jnp.concatenate(pieces, axis=1)
    for index in range(pack.spare):
        chunk, place = pack.tail_place(pack.tail_tiles + index)
        buf[slots[chunk], :, place : place + LANES] = jnp.zeros((own, LANES), jnp.float32)
    at = 0
    for low, high in cuts:
        for slot in range(pack.members):
            outs[at][...] = buf[slot, :, low:high]
            at += 1


def packed(pack, cuts, me, cells, after=()):
    own = cells.shape[2]
    outs = call(
        functools.partial(pack_body, pack, cuts),
        out_shape=[
            held((own, high - low), pltpu.HBM)
            for low, high in cuts
            for _ in range(pack.members)
        ],
        in_specs=[SMEM, VMEM],
        out_specs=[VMEM] * (len(cuts) * pack.members),
        operands=[me, cells],
        scratch_shapes=[pltpu.VMEM((pack.members, own, pack.lanes), jnp.float32)],
        after=after,
    )
    return [outs[i * pack.members : (i + 1) * pack.members] for i in range(len(cuts))]


def unpack_body(pack, cuts, me_ref, *refs):
    parts, out_ref, buf = refs[:-2], refs[-2], refs[-1]
    me = me_ref[0]
    at = 0
    for low, high in cuts:
        for shift in range(pack.members):
            chunk = lax.rem(me - shift + pack.members, pack.members)
            buf[chunk, :, low:high] = parts[at][...]
            at += 1
    for row in range(pack.rows):
        x, z = divmod(row, pack.depth)
        for chunk, there, here, count in pack.runs(row):
            out_ref[x, z, :, here : here + count] = buf[chunk, :, there : there + count]
    start = pack.full * LANES
    for index in range(pack.tail_tiles):
        chunk, place = pack.tail_place(index)
        tile = buf[chunk, :, place : place + LANES]
        for k, row in enumerate(range(index * pack.group, min(pack.rows, (index + 1) * pack.group))):
            x, z = divmod(row, pack.depth)
            out_ref[x, z, :, start : start + pack.tail] = tile[:, k * pack.tail : (k + 1) * pack.tail]


def unpacked(pack, cuts, me, parts, after=()):
    own = parts[0].shape[0]
    return call(
        functools.partial(unpack_body, pack, cuts),
        out_shape=[jax.ShapeDtypeStruct((pack.width, pack.depth, own, pack.across), jnp.float32)],
        in_specs=[SMEM] + [VMEM] * len(parts),
        out_specs=[VMEM],
        operands=[me, *parts],
        scratch_shapes=[pltpu.VMEM((pack.members, own, pack.lanes), jnp.float32)],
        after=after,
    )


def distance_body(members, me_ref, *refs):
    parts, out_ref, all_ref = refs[:members], refs[members], refs[members + 1]
    own = parts[0].shape[0]
    me = me_ref[0]
    for shift in range(members):
        row = pl.multiple_of(lax.rem(me - shift + members, members) * own, own)
        all_ref[pl.ds(row, own), :] = parts[shift][...]
    cells = all_ref[...]
    cells = cells - cells[0:1, :]
    gram = lax.dot_general(
        cells,
        cells,
        (((1,), (1,)), ((), ())),
        precision=lax.Precision.HIGHEST,
        preferred_element_type=jnp.float32,
    )
    count = gram.shape[0]
    rows = lax.broadcasted_iota(jnp.int32, (count, count), 0)
    cols = lax.broadcasted_iota(jnp.int32, (count, count), 1)
    diag = jnp.where(rows == cols, gram, 0.0)
    down = jnp.sum(diag, axis=1, keepdims=True)
    along = jnp.sum(diag, axis=0, keepdims=True)
    dist = jnp.where(rows == cols, 0.0, down + along - 2.0 * gram)
    for member in range(members):
        out_ref[:, member * count : (member + 1) * count] = dist[member * own : (member + 1) * own]


def distances(members, me, parts, after=()):
    own, lanes = parts[0].shape
    count = own * members
    return call(
        functools.partial(distance_body, members),
        out_shape=[held((own, members * count))],
        in_specs=[SMEM] + [VMEM] * members,
        out_specs=[VMEM],
        operands=[me, *parts],
        scratch_shapes=[pltpu.VMEM((count, lanes), jnp.float32)],
        after=after,
    )


def update_body(members, low, me_ref, dist_ref, *refs):
    cells, grads = refs[:members], refs[members : 2 * members]
    outs = refs[2 * members : 3 * members]
    cell_ref, grad_ref, out_ref = refs[3 * members :]
    own, lanes = grads[0].shape
    count = own * members
    me = me_ref[0]
    for shift in range(members):
        row = pl.multiple_of(lax.rem(me - shift + members, members) * own, own)
        cell_ref[pl.ds(row, own), :] = cells[shift][:, low : low + lanes]
        grad_ref[pl.ds(row, own), :] = grads[shift][...]
    dist = jnp.concatenate(
        [dist_ref[:, member * count : (member + 1) * count] for member in range(members)], axis=0
    )
    band = jnp.sum(jnp.sum(dist, axis=1, keepdims=True), axis=0, keepdims=True) / (
        count * (count - 1) * math.log(count + 1)
    )
    kern = jnp.exp(-dist / band)
    total = jnp.sum(kern, axis=1, keepdims=True)
    cell = cell_ref[...]
    mixed = 0.5 * band * grad_ref[...] - cell
    pulled = jnp.dot(
        kern, mixed, precision=lax.Precision.HIGHEST, preferred_element_type=jnp.float32
    )
    out_ref[...] = cell + step_size * (pulled + total * cell)
    for shift in range(members):
        row = pl.multiple_of(lax.rem(me + shift, members) * own, own)
        outs[shift][...] = out_ref[pl.ds(row, own), :]


def updated(members, low, me, dist, cells, grads, after=()):
    own, lanes = grads[0].shape
    count = own * members
    return call(
        functools.partial(update_body, members, low),
        out_shape=[held((own, lanes), pltpu.HBM)] * members,
        in_specs=[SMEM, VMEM] + [VMEM] * (2 * members),
        out_specs=[VMEM] * members,
        operands=[me, dist, *cells, *grads],
        scratch_shapes=[pltpu.VMEM((count, lanes), jnp.float32)] * 3,
        after=after,
    )


def exchange(parts, members):
    return [parts[0]] + [
        lax.ppermute(parts[shift], "member", [(i, (i + shift) % members) for i in range(members)])
        for shift in range(1, members)
    ]


def spread_rows(across, cells_ref, out_ref):
    width, depth, own, lanes = out_ref.shape
    start = (across // LANES) * LANES
    if lanes > start:
        edge = jnp.zeros((own, lanes - start), jnp.float32)

    def one(x, carry):
        for z in range(depth):
            if lanes > start:
                out_ref[x, z, :, start:] = edge
            out_ref[x, z, :, :across] = cells_ref[x, z]
        return carry

    lax.fori_loop(0, width, one, 0)


def spread_body(across, now_ref, out_ref, head_ref, tail_ref):
    width = now_ref.shape[0]
    spread_rows(across, now_ref, out_ref)
    head_ref[...] = out_ref[0:GHOST]
    tail_ref[...] = out_ref[width - GHOST :]


def spread(across, lanes, now, after=()):
    out = held(now.shape[:3] + (lanes,))
    edge = held((GHOST,) + now.shape[1:3] + (lanes,))
    return call(
        functools.partial(spread_body, across),
        out_shape=[out, edge, edge],
        in_specs=[VMEM],
        out_specs=[VMEM] * 3,
        operands=[now],
        after=after,
    )


def medium_body(across, cells_ref, ghosts_ref, prev_ref, coef_ref, still_ref, wide_ref):
    width, depth, own, _ = cells_ref.shape
    lanes = coef_ref.shape[-1]
    start = (across // LANES) * LANES
    spread_rows(across, prev_ref, wide_ref)
    if lanes > start:
        edge = jnp.zeros((own, lanes - start), jnp.float32)

    def one(x, carry):
        for z in range(depth):
            if lanes > start:
                coef_ref[x, z, :, start:] = edge
                still_ref[x, z, :, start:] = edge
            speed = courant * (1.0 + 0.3 * jnp.tanh(cells_ref[x, z]))
            coef_ref[x, z, :, :across] = speed * speed
            total = None
            for offset in range(1, GHOST + 1):
                terms = []
                if z - offset < 0:
                    terms.append(ghosts_ref[x, GHOST + z - offset])
                if z + offset >= depth:
                    terms.append(ghosts_ref[x, GHOST + z + offset - depth])
                for term in terms:
                    part = weights[offset] * term
                    total = part if total is None else total + part
            if total is None:
                total = jnp.zeros((own, across), jnp.float32)
            still_ref[x, z, :, :across] = total
        return carry

    lax.fori_loop(0, width, one, 0)


def medium(across, lanes, cells, ghosts, prev, after=()):
    shape = held(cells.shape[:3] + (lanes,))
    return call(
        functools.partial(medium_body, across),
        out_shape=[shape] * 3,
        in_specs=[VMEM] * 3,
        out_specs=[VMEM] * 3,
        operands=[cells, ghosts, prev],
        after=after,
    )


def wave_body(amplitude, last, spot_ref, left_ref, right_ref, now_ref, prev_ref, coef_ref, still_ref, *refs):
    out_ref, wide = refs[0], refs[-1]
    width, depth, own, lanes = now_ref.shape
    wide[0:GHOST] = left_ref[...]
    wide[GHOST : GHOST + width] = now_ref[...]
    wide[GHOST + width :] = right_ref[...]
    cols = lax.broadcasted_iota(jnp.int32, (own, lanes), 1)
    spot = jnp.broadcast_to(spot_ref[:, 0:1], (own, lanes)) - cols

    def one(x, carry):
        for z in range(depth):
            center = wide[x + GHOST, z]
            total = 3.0 * weights[0] * center + still_ref[x, z]
            for offset in range(1, GHOST + 1):
                pair = wide[x + GHOST + offset, z] + wide[x + GHOST - offset, z]
                pair = pair + pltpu.roll(center, offset, 1) + pltpu.roll(center, lanes - offset, 1)
                if z - offset >= 0:
                    pair = pair + wide[x + GHOST, z - offset]
                if z + offset < depth:
                    pair = pair + wide[x + GHOST, z + offset]
                total = total + weights[offset] * pair
            value = 2.0 * center - prev_ref[x, z] + coef_ref[x, z] * total
            if z == 0:
                value = value + jnp.where(spot == x * lanes, amplitude, 0.0)
            out_ref[x, z] = value
        return carry

    lax.fori_loop(0, width, one, 0)
    if not last:
        head_ref, tail_ref = refs[1], refs[2]
        head_ref[...] = out_ref[0:GHOST]
        tail_ref[...] = out_ref[width - GHOST :]


def wave_step(amplitude, last, spot, left, right, now, prev, coef, still, after=()):
    width, depth, own, lanes = now.shape
    out = held(now.shape)
    edge = held((GHOST,) + now.shape[1:])
    outs = [out] if last else [out, edge, edge]
    return call(
        functools.partial(wave_body, amplitude, last),
        out_shape=outs,
        in_specs=[VMEM] * 7,
        out_specs=[VMEM] * len(outs),
        operands=[spot, left, right, now, prev, coef, still],
        scratch_shapes=[pltpu.VMEM((width + 2 * GHOST, depth, own, lanes), jnp.float32)],
        after=after,
    )


def shards(cuts_of, particles, loglik_grad, wave_prev, wave_now, ghosts, src_cell):
    own, depth, width, across = particles.shape
    members = lax.axis_size("member")
    spaces = lax.axis_size("space")
    member_idx = lax.axis_index("member")
    space_idx = lax.axis_index("space")
    pack = Packing(width, depth, across, members)
    whole = [(0, pack.lanes)]
    cuts = cuts_of(pack)
    me = jnp.reshape(member_idx, (1,)).astype(jnp.int32)
    lanes = -(-(across + GHOST) // LANES) * LANES

    def turned(array):
        return jnp.transpose(array, (2, 1, 0, 3))

    cells = turned(particles)
    ready = packed(pack, whole, me, cells)[0]
    ready, loglik_grad, wave_prev, wave_now, ghosts, src_cell = lax.optimization_barrier(
        (ready, loglik_grad, wave_prev, wave_now, ghosts, src_cell)
    )
    cell_parts = exchange(ready, members)

    now, head, tail = spread(across, lanes, turned(wave_now))
    spot = (src_cell // across - space_idx * width) * lanes + src_cell % across
    spot = jnp.broadcast_to(spot[:, None], (own, LANES))
    coef, still, prev = medium(across, lanes, cells, turned(ghosts), turned(wave_prev), after=[now])
    waves = [prev, now]

    def step(index, head, tail, after):
        left = lax.ppermute(tail, "space", [(i, i + 1) for i in range(spaces - 1)])
        right = lax.ppermute(head, "space", [(i + 1, i) for i in range(spaces - 1)])
        outs = wave_step(
            2.0 * math.cos(1.3 * index), index == STEPS - 1, spot, left, right,
            waves[-1], waves[-2], coef, still, after=after,
        )
        waves.append(outs[0])
        return outs[1:]

    edges = step(0, head, tail, [])
    grads = packed(pack, cuts, me, turned(loglik_grad), after=[waves[-1]])
    grad_parts = [exchange(part, members) for part in grads]
    dist = distances(members, me, cell_parts, after=[waves[-1]])[0]
    dist = jnp.sum(lax.all_gather(dist, "space", axis=0), axis=0)
    edges = step(1, *edges, after=[dist])
    dist = sum(exchange([dist] * members, members))

    moved = []
    order = waves[-1]
    for (low, _), grads in zip(cuts, grad_parts):
        out = updated(members, low, me, dist, cell_parts, grads, after=[order])
        order = out[0]
        moved += exchange(out, members)
    for index in range(2, STEPS):
        edges = step(index, *edges, after=[order])
    ends = [jnp.transpose(wave[..., :across], (2, 0, 1, 3)) for wave in waves[-2:]]
    new_particles = turned(unpacked(pack, cuts, me, moved, after=ends)[0])
    return new_particles, *[jnp.transpose(end, (0, 2, 1, 3)) for end in ends]


def one_cut(pack):
    return [(0, pack.lanes)]


def solution(mesh):
    spec = P("member", None, "space", None)
    return jax.shard_map(
        functools.partial(shards, one_cut),
        mesh=mesh,
        in_specs=(spec, spec, spec, spec, spec, P("member")),
        out_specs=(spec, spec, spec),
        check_vma=False,
    )
```

profile of v0, /device:TPU:12, one launch (start us, length us, event | category | flops | bytes accessed | tf_op | source)
XLA Modules:
  0.0 124.6 jit_solution(14696618553374831488)
XLA Ops:
  0.6 1.6 %copy.27 = f32[8,2,25,800]{3,0,1,2:T(8,128)S(1)} copy(f32[8,2,25,800]{3,1,2,0:T(2,128)} %param.6) | data formatting | bytes 2560000 | tf_op args[0]
  2.2 1.2 shard_map.85
  3.4 1.6 %collective-permute-start = (f32[8,10112]{1,0:T(8,128)}, f32[8,10112]{1,0:T(8,128)S(1)}, u32[]{:S(2)}, u32[]{:S(2)}) collective-permute-start(f32[8,10112]{1,0:T(8,128)} %get-tuple-element.44), channel_id=1, source_target_pairs={{0,8},{8,16},{16,24},{24,0},{1,9},{9,17},{17,25},{25,1},{2,10},{10... | collective-permute-start | bytes 970760 | tf_op jit(solution)/shard_map/ppermute | solution.py:243
  5.0 1.2 collective-permute-start.1
  6.3 1.8 %collective-permute-start.2 = (f32[8,10112]{1,0:T(8,128)}, f32[8,10112]{1,0:T(8,128)}, u32[]{:S(2)}, u32[]{:S(2)}) collective-permute-start(f32[8,10112]{1,0:T(8,128)} %get-tuple-element.46), channel_id=1, source_target_pairs={{0,24},{8,0},{16,8},{24,16},{1,25},{9,1},{17,9},{25,17},{2,26},{10... | collective-permute-start | bytes 970760 | tf_op jit(solution)/shard_map/ppermute | solution.py:243
  8.1 1.3 %copy_bitcast_fusion.2 = (f32[25,2,8,800]{3,2,1,0:T(8,128)}, f32[25,2,8,800]{3,2,1,0:T(8,128)S(1)}) fusion(f32[8,2,25,800]{3,1,2,0:T(2,128)S(1)} %copy-done.8, f32[8,2,25,800]{3,1,2,0:T(2,128)S(1)} %copy-done.9), kind=kLoop, calls=%fused_computation.2 | loop fusion | bytes 5120000 | tf_op jit(solution)/shard_map/transpose | solution.py:392
  10.4 2.0 %collective-permute-start.3 = (f32[4,2,8,896]{3,2,1,0:T(8,128)}, f32[4,2,8,896]{3,2,1,0:T(8,128)}, u32[]{:S(2)}, u32[]{:S(2)}) collective-permute-start(f32[4,2,8,896]{3,2,1,0:T(8,128)} %get-tuple-element.49), channel_id=1, source_target_pairs={{0,1},{1,2},{2,3},{3,4},{4,5},{5,6},{6,7},{8,9},{9,10},{10,11},{11... | collective-permute-start | bytes 688136 | tf_op jit(solution)/shard_map/ppermute | solution.py:408
  12.4 4.5 %collective-permute-start.4 = (f32[4,2,8,896]{3,2,1,0:T(8,128)}, f32[4,2,8,896]{3,2,1,0:T(8,128)}, u32[]{:S(2)}, u32[]{:S(2)}) collective-permute-start(f32[4,2,8,896]{3,2,1,0:T(8,128)} %get-tuple-element.50), channel_id=1, source_target_pairs={{1,0},{2,1},{3,2},{4,3},{5,4},{6,5},{7,6},{9,8},{10,9},{11,10},{12... | collective-permute-start | bytes 688136 | tf_op jit(solution)/shard_map/ppermute | solution.py:409
  17.0 3.5 %copy.25 = f32[8,8,25,800]{3,0,1,2:T(8,128)} copy(f32[8,8,25,800]{3,1,2,0:T(8,128)S(1)} %copy-done.6) | data formatting | bytes 10240000 | tf_op jit(solution)/shard_map/optimization_barrier | solution.py:396
  20.4 2.6 %copy-done = f32[8,8,25,800]{3,0,1,2:T(8,128)S(1)} copy-done((f32[8,8,25,800]{3,0,1,2:T(8,128)S(1)}, f32[8,8,25,800]{3,0,1,2:T(8,128)}, u32[]{:S(2)}) %copy-start) | copy-done | bytes 5120024
  23.1 1.4 %copy-done.2 = f32[25,2,8,800]{3,2,1,0:T(8,128)S(1)} copy-done((f32[25,2,8,800]{3,2,1,0:T(8,128)S(1)}, f32[25,2,8,800]{3,2,1,0:T(8,128)}, u32[]{:S(2)}) %copy-start.2) | copy-done | bytes 1280024
  24.4 1.2 shard_map.87
  25.8 6.2 %shard_map.88 = (f32[25,2,8,896]{3,2,1,0:T(8,128)S(1)}, f32[4,2,8,896]{3,2,1,0:T(8,128)S(1)}, f32[4,2,8,896]{3,2,1,0:T(8,128)S(1)}) custom-call(s32[8,128]{1,0:T(8,128)S(1)} %broadcast_in_dim.2.refs_0_, f32[4,2,8,896]{3,2,1,0:T(8,128)} %collective-permute-done.3.refs_1_, f32[4,2,8,896]{3,2,1,0:T(8,128)} %collective-permute-done.4.refs_2_, ...), custom_call_target="tpu_custom_call" | custom-call | tf_op jit(solution)/shard_map/pallas_call | solution.py:37
  32.0 2.1 %collective-permute-start.11 = (f32[4,2,8,896]{3,2,1,0:T(8,128)S(1)}, f32[4,2,8,896]{3,2,1,0:T(8,128)S(1)}, u32[]{:S(2)}, u32[]{:S(2)}) collective-permute-start(f32[4,2,8,896]{3,2,1,0:T(8,128)S(1)} %get-tuple-element.63), channel_id=1, source_target_pairs={{0,1},{1,2},{2,3},{3,4},{4,5},{5,6},{6,7},{8,9},{9,10},{10,11},{11... | collective-permute-start | bytes 688136 | tf_op jit(solution)/shard_map/ppermute | solution.py:408
  34.0 4.5 %collective-permute-start.12 = (f32[4,2,8,896]{3,2,1,0:T(8,128)S(1)}, f32[4,2,8,896]{3,2,1,0:T(8,128)S(1)}, u32[]{:S(2)}, u32[]{:S(2)}) collective-permute-start(f32[4,2,8,896]{3,2,1,0:T(8,128)S(1)} %get-tuple-element.64), channel_id=1, source_target_pairs={{1,0},{2,1},{3,2},{4,3},{5,4},{6,5},{7,6},{9,8},{10,9},{11,10},{12... | collective-permute-start | bytes 688136 | tf_op jit(solution)/shard_map/ppermute | solution.py:409
  38.6 2.3 %shard_map.89 = f32[8,128]{1,0:T(8,128)S(1)} custom-call(s32[1]{0:T(128)} %bitcast.refs_0_, f32[8,10112]{1,0:T(8,128)S(1)} %copy-done.4, f32[8,10112]{1,0:T(8,128)S(1)} %collective-permute-done.refs_2_.refs_3_, f32[8,10112]{1,0:T(8,128)S(1)} %collective-permute-done.1.refs_3_.refs_4_, f32[8,10112]{1,0:T(8,128)} %collective-permute-done.2.refs_4_.refs_5_, ...), custom_call_target="tpu_custom_call" | custom-call | tf_op jit(solution)/shard_map/pallas_call | solution.py:37
  40.9 7.3 %all-gather = f32[64,128]{1,0:T(8,128)S(1)} all-gather(f32[8,128]{1,0:T(8,128)S(1)} %shard_map.89), channel_id=2, replica_groups=mesh['member'=4,'space'=8] {'space'}, dimensions={0}, use_global_device_ids=true | all-gather | bytes 36864 | tf_op jit(solution)/shard_map/all_gather | solution.py:421
  49.8 1.8 %collective-permute-start.10 = (f32[8,10112]{1,0:T(8,128)}, f32[8,10112]{1,0:T(8,128)S(1)}, u32[]{:S(2)}, u32[]{:S(2)}) collective-permute-start(f32[8,10112]{1,0:T(8,128)} %get-tuple-element.62), channel_id=1, source_target_pairs={{0,24},{8,0},{16,8},{24,16},{1,25},{9,1},{17,9},{25,17},{2,26},{10... | collective-permute-start | bytes 970760 | tf_op jit(solution)/shard_map/ppermute | solution.py:243
  51.8 5.2 %collective-permute-start.9 = (f32[8,10112]{1,0:T(8,128)}, f32[8,10112]{1,0:T(8,128)S(1)}, u32[]{:S(2)}, u32[]{:S(2)}) collective-permute-start(f32[8,10112]{1,0:T(8,128)} %get-tuple-element.61), channel_id=1, source_target_pairs={{0,16},{8,24},{16,0},{24,8},{1,17},{9,25},{17,1},{25,9},{2,18},{10... | collective-permute-start | bytes 970760 | tf_op jit(solution)/shard_map/ppermute | solution.py:243
  57.9 5.1 %shard_map.91 = (f32[25,2,8,896]{3,2,1,0:T(8,128)S(1)}, f32[4,2,8,896]{3,2,1,0:T(8,128)S(1)}, f32[4,2,8,896]{3,2,1,0:T(8,128)S(1)}) custom-call(s32[8,128]{1,0:T(8,128)S(1)} %broadcast_in_dim.2.refs_0_, f32[4,2,8,896]{3,2,1,0:T(8,128)S(1)} %collective-permute-done.11.refs_1_, f32[4,2,8,896]{3,2,1,0:T(8,128)S(1)} %collective-permute-done.12.refs_2_, ...), custom_call_target="tpu_custom_call" | custom-call | tf_op jit(solution)/shard_map/pallas_call | solution.py:37
  63.0 17.1 %collective-permute-done.6 = f32[8,128]{1,0:T(8,128)S(1)} collective-permute-done((f32[8,128]{1,0:T(8,128)S(1)}, f32[8,128]{1,0:T(8,128)S(1)}, u32[]{:S(2)}, u32[]{:S(2)}) %collective-permute-start.6) | collective-permute-done | bytes 4128 | tf_op jit(solution)/shard_map/ppermute | solution.py:243
  80.1 1.9 %collective-permute-start.16 = (f32[4,2,8,896]{3,2,1,0:T(8,128)S(1)}, f32[4,2,8,896]{3,2,1,0:T(8,128)S(1)}, u32[]{:S(2)}, u32[]{:S(2)}) collective-permute-start(f32[4,2,8,896]{3,2,1,0:T(8,128)S(1)} %get-tuple-element.70), channel_id=1, source_target_pairs={{0,1},{1,2},{2,3},{3,4},{4,5},{5,6},{6,7},{8,9},{9,10},{10,11},{11... | collective-permute-start | bytes 688136 | tf_op jit(solution)/shard_map/ppermute | solution.py:408
  82.0 4.5 %collective-permute-start.17 = (f32[4,2,8,896]{3,2,1,0:T(8,128)S(1)}, f32[4,2,8,896]{3,2,1,0:T(8,128)S(1)}, u32[]{:S(2)}, u32[]{:S(2)}) collective-permute-start(f32[4,2,8,896]{3,2,1,0:T(8,128)S(1)} %get-tuple-element.71), channel_id=1, source_target_pairs={{1,0},{2,1},{3,2},{4,3},{5,4},{6,5},{7,6},{9,8},{10,9},{11,10},{12... | collective-permute-start | bytes 688136 | tf_op jit(solution)/shard_map/ppermute | solution.py:409
  86.6 3.6 %shard_map.92 = (f32[8,10112]{1,0:T(8,128)}, f32[8,10112]{1,0:T(8,128)}, f32[8,10112]{1,0:T(8,128)}, f32[8,10112]{1,0:T(8,128)}) custom-call(s32[1]{0:T(128)} %bitcast.refs_0_, f32[8,128]{1,0:T(8,128)S(1)} %add_add_fusion.refs_1_, f32[8,10112]{1,0:T(8,128)S(1)} %copy-done.4, f32[8,10112]{1,0:T(8,128)S(1)} %collective-permute-done.refs_2_.refs_3_, ...), custom_call_target="tpu_custom_call" | custom-call | tf_op jit(solution)/shard_map/pallas_call | solution.py:37
  90.6 4.2 %collective-permute-start.14 = (f32[8,10112]{1,0:T(8,128)}, f32[8,10112]{1,0:T(8,128)S(1)}, u32[]{:S(2)}, u32[]{:S(2)}) collective-permute-start(f32[8,10112]{1,0:T(8,128)} %get-tuple-element.68), channel_id=1, source_target_pairs={{0,16},{8,24},{16,0},{24,8},{1,17},{9,25},{17,1},{25,9},{2,18},{10... | collective-permute-start | bytes 970760 | tf_op jit(solution)/shard_map/ppermute | solution.py:243
  96.5 5.1 %shard_map.93 = (f32[25,2,8,896]{3,2,1,0:T(8,128)S(1)}, f32[4,2,8,896]{3,2,1,0:T(8,128)S(1)}, f32[4,2,8,896]{3,2,1,0:T(8,128)S(1)}) custom-call(s32[8,128]{1,0:T(8,128)S(1)} %broadcast_in_dim.2.refs_0_, f32[4,2,8,896]{3,2,1,0:T(8,128)S(1)} %collective-permute-done.16.refs_1_, f32[4,2,8,896]{3,2,1,0:T(8,128)S(1)} %collective-permute-done.17.refs_2_, ...), custom_call_target="tpu_custom_call" | custom-call | tf_op jit(solution)/shard_map/pallas_call | solution.py:37
  101.6 1.9 %collective-permute-start.18 = (f32[4,2,8,896]{3,2,1,0:T(8,128)S(1)}, f32[4,2,8,896]{3,2,1,0:T(8,128)S(1)}, u32[]{:S(2)}, u32[]{:S(2)}) collective-permute-start(f32[4,2,8,896]{3,2,1,0:T(8,128)S(1)} %get-tuple-element.73), channel_id=1, source_target_pairs={{0,1},{1,2},{2,3},{3,4},{4,5},{5,6},{6,7},{8,9},{9,10},{10,11},{11... | collective-permute-start | bytes 688136 | tf_op jit(solution)/shard_map/ppermute | solution.py:408
  103.5 4.5 %collective-permute-start.19 = (f32[4,2,8,896]{3,2,1,0:T(8,128)S(1)}, f32[4,2,8,896]{3,2,1,0:T(8,128)S(1)}, u32[]{:S(2)}, u32[]{:S(2)}) collective-permute-start(f32[4,2,8,896]{3,2,1,0:T(8,128)S(1)} %get-tuple-element.74), channel_id=1, source_target_pairs={{1,0},{2,1},{3,2},{4,3},{5,4},{6,5},{7,6},{9,8},{10,9},{11,10},{12... | collective-permute-start | bytes 688136 | tf_op jit(solution)/shard_map/ppermute | solution.py:409
  108.8 1.8 %slice_bitcast_fusion = (f32[8,2,25,800]{3,1,2,0:T(2,128)}, f32[8,25,2,800]{3,2,1,0:T(2,128)S(1)}) fusion(f32[25,2,8,896]{3,1,0,2:T(2,128)S(1)} %copy.14), kind=kLoop, calls=%fused_computation.5 | loop fusion | bytes 3840000 | tf_op jit(solution)/shard_map/transpose;transpose | solution.py:435
  111.6 5.0 %shard_map.94 = f32[25,2,8,896]{3,2,1,0:T(8,128)S(1)} custom-call(s32[8,128]{1,0:T(8,128)S(1)} %broadcast_in_dim.2.refs_0_, f32[4,2,8,896]{3,2,1,0:T(8,128)S(1)} %collective-permute-done.18.refs_1_, f32[4,2,8,896]{3,2,1,0:T(8,128)S(1)} %collective-permute-done.19.refs_2_, f32[25,2,8,896]{3,2,1,0:T(8,128)S(1)} %get-tuple-element.72.refs_3_, ...), custom_call_target="tpu_custom_call" | custom-call | tf_op jit(solution)/shard_map/pallas_call | solution.py:37
  118.5 3.9 %collective-permute-done.15.refs_4_ = f32[8,10112]{1,0:T(8,128)S(1)} collective-permute-done((f32[8,10112]{1,0:T(8,128)}, f32[8,10112]{1,0:T(8,128)S(1)}, u32[]{:S(2)}, u32[]{:S(2)}) %collective-permute-start.15) | collective-permute-done | bytes 323616 | tf_op jit(solution)/shard_map/ppermute | solution.py:243
  122.7 1.8 %copy.16 = f32[8,2,25,800]{3,1,2,0:T(2,128)} copy(f32[8,2,25,800]{3,0,1,2:T(8,128)S(1)} %bitcast.34) | data formatting | bytes 2560000
  (54 shorter events, 9.8 us)
Async XLA Ops:
  0.6 7.4 %copy-start.9 = (f32[8,2,25,800]{3,1,2,0:T(2,128)S(1)}, f32[8,2,25,800]{3,1,2,0:T(2,128)}, u32[]{:S(2)}) copy-start(f32[8,2,25,800]{3,1,2,0:T(2,128)} %param.9) | copy-start | bytes 3840004
  2.2 5.8 %copy-start.8 = (f32[8,2,25,800]{3,1,2,0:T(2,128)S(1)}, f32[8,2,25,800]{3,1,2,0:T(2,128)}, u32[]{:S(2)}) copy-start(f32[8,2,25,800]{3,1,2,0:T(2,128)} %param.8) | copy-start | bytes 3840004
  3.4 35.2 %collective-permute-start = (f32[8,10112]{1,0:T(8,128)}, f32[8,10112]{1,0:T(8,128)S(1)}, u32[]{:S(2)}, u32[]{:S(2)}) collective-permute-start(f32[8,10112]{1,0:T(8,128)} %get-tuple-element.44), channel_id=1, source_target_pairs={{0,8},{8,16},{16,24},{24,0},{1,9},{9,17},{17,25},{25,1},{2,10},{10... | collective-permute-start | bytes 970760 | tf_op jit(solution)/shard_map/ppermute | solution.py:243
  5.0 33.6 %collective-permute-start.1 = (f32[8,10112]{1,0:T(8,128)}, f32[8,10112]{1,0:T(8,128)S(1)}, u32[]{:S(2)}, u32[]{:S(2)}) collective-permute-start(f32[8,10112]{1,0:T(8,128)} %get-tuple-element.45), channel_id=1, source_target_pairs={{0,16},{8,24},{16,0},{24,8},{1,17},{9,25},{17,1},{25,9},{2,18},{10... | collective-permute-start | bytes 970760 | tf_op jit(solution)/shard_map/ppermute | solution.py:243
  6.3 32.4 %collective-permute-start.2 = (f32[8,10112]{1,0:T(8,128)}, f32[8,10112]{1,0:T(8,128)}, u32[]{:S(2)}, u32[]{:S(2)}) collective-permute-start(f32[8,10112]{1,0:T(8,128)} %get-tuple-element.46), channel_id=1, source_target_pairs={{0,24},{8,0},{16,8},{24,16},{1,25},{9,1},{17,9},{25,17},{2,26},{10... | collective-permute-start | bytes 970760 | tf_op jit(solution)/shard_map/ppermute | solution.py:243
  8.1 8.9 %copy-start.6 = (f32[8,8,25,800]{3,1,2,0:T(8,128)S(1)}, f32[8,8,25,800]{3,1,2,0:T(8,128)}, u32[]{:S(2)}) copy-start(f32[8,8,25,800]{3,1,2,0:T(8,128)} %param.10) | copy-start | bytes 15360004
  10.4 15.4 %collective-permute-start.3 = (f32[4,2,8,896]{3,2,1,0:T(8,128)}, f32[4,2,8,896]{3,2,1,0:T(8,128)}, u32[]{:S(2)}, u32[]{:S(2)}) collective-permute-start(f32[4,2,8,896]{3,2,1,0:T(8,128)} %get-tuple-element.49), channel_id=1, source_target_pairs={{0,1},{1,2},{2,3},{3,4},{4,5},{5,6},{6,7},{8,9},{9,10},{10,11},{11... | collective-permute-start | bytes 688136 | tf_op jit(solution)/shard_map/ppermute | solution.py:408
  12.4 13.3 %collective-permute-start.4 = (f32[4,2,8,896]{3,2,1,0:T(8,128)}, f32[4,2,8,896]{3,2,1,0:T(8,128)}, u32[]{:S(2)}, u32[]{:S(2)}) collective-permute-start(f32[4,2,8,896]{3,2,1,0:T(8,128)} %get-tuple-element.50), channel_id=1, source_target_pairs={{1,0},{2,1},{3,2},{4,3},{5,4},{6,5},{7,6},{9,8},{10,9},{11,10},{12... | collective-permute-start | bytes 688136 | tf_op jit(solution)/shard_map/ppermute | solution.py:409
  20.4 2.6 %copy-start = (f32[8,8,25,800]{3,0,1,2:T(8,128)S(1)}, f32[8,8,25,800]{3,0,1,2:T(8,128)}, u32[]{:S(2)}) copy-start(f32[8,8,25,800]{3,0,1,2:T(8,128)} %copy.25) | copy-start | bytes 15360004
  23.1 1.4 %copy-start.2 = (f32[25,2,8,800]{3,2,1,0:T(8,128)S(1)}, f32[25,2,8,800]{3,2,1,0:T(8,128)}, u32[]{:S(2)}) copy-start(f32[25,2,8,800]{3,2,1,0:T(8,128)} %get-tuple-element.82.refs_2_) | copy-start | bytes 3840004
  24.4 1.3 %copy-start.10 = (s32[8]{0:T(128)S(1)}, s32[8]{0:T(128)}, u32[]{:S(2)}) copy-start(s32[8]{0:T(128)} %param.11) | copy-start | bytes 100
  25.8 12.8 %copy-start.4 = (f32[8,10112]{1,0:T(8,128)S(1)}, f32[8,10112]{1,0:T(8,128)}, u32[]{:S(2)}) copy-start(f32[8,10112]{1,0:T(8,128)} %get-tuple-element.43.refs_1_.refs_2_) | copy-start | bytes 970756
  32.0 16.5 %copy-start.7 = (f32[8,2,25,800]{3,1,2,0:T(2,128)S(1)}, f32[8,2,25,800]{3,1,2,0:T(2,128)}, u32[]{:S(2)}) copy-start(f32[8,2,25,800]{3,1,2,0:T(2,128)} %param.7) | copy-start | bytes 3840004
  32.0 25.1 %collective-permute-start.11 = (f32[4,2,8,896]{3,2,1,0:T(8,128)S(1)}, f32[4,2,8,896]{3,2,1,0:T(8,128)S(1)}, u32[]{:S(2)}, u32[]{:S(2)}) collective-permute-start(f32[4,2,8,896]{3,2,1,0:T(8,128)S(1)} %get-tuple-element.63), channel_id=1, source_target_pairs={{0,1},{1,2},{2,3},{3,4},{4,5},{5,6},{6,7},{8,9},{9,10},{10,11},{11... | collective-permute-start | bytes 688136 | tf_op jit(solution)/shard_map/ppermute | solution.py:408
  34.0 23.1 %collective-permute-start.12 = (f32[4,2,8,896]{3,2,1,0:T(8,128)S(1)}, f32[4,2,8,896]{3,2,1,0:T(8,128)S(1)}, u32[]{:S(2)}, u32[]{:S(2)}) collective-permute-start(f32[4,2,8,896]{3,2,1,0:T(8,128)S(1)} %get-tuple-element.64), channel_id=1, source_target_pairs={{1,0},{2,1},{3,2},{4,3},{5,4},{6,5},{7,6},{9,8},{10,9},{11,10},{12... | collective-permute-start | bytes 688136 | tf_op jit(solution)/shard_map/ppermute | solution.py:409
  48.2 3.6 %collective-permute-start.5 = (f32[8,128]{1,0:T(8,128)S(1)}, f32[8,128]{1,0:T(8,128)S(1)}, u32[]{:S(2)}, u32[]{:S(2)}) collective-permute-start(f32[8,128]{1,0:T(8,128)S(1)} %bitcast_reduce_fusion.refs_7_), channel_id=1, source_target_pairs={{0,8},{8,16},{16,24},{24,0},{1,9},{9,17},{17,25},{25,1},{2,10},{10... | collective-permute-start | bytes 12296 | tf_op jit(solution)/shard_map/ppermute | solution.py:243
  49.8 36.8 %collective-permute-start.10 = (f32[8,10112]{1,0:T(8,128)}, f32[8,10112]{1,0:T(8,128)S(1)}, u32[]{:S(2)}, u32[]{:S(2)}) collective-permute-start(f32[8,10112]{1,0:T(8,128)} %get-tuple-element.62), channel_id=1, source_target_pairs={{0,24},{8,0},{16,8},{24,16},{1,25},{9,1},{17,9},{25,17},{2,26},{10... | collective-permute-start | bytes 970760 | tf_op jit(solution)/shard_map/ppermute | solution.py:243
  51.6 35.0 %collective-permute-start.8 = (f32[8,10112]{1,0:T(8,128)}, f32[8,10112]{1,0:T(8,128)S(1)}, u32[]{:S(2)}, u32[]{:S(2)}) collective-permute-start(f32[8,10112]{1,0:T(8,128)} %get-tuple-element.60), channel_id=1, source_target_pairs={{0,8},{8,16},{16,24},{24,0},{1,9},{9,17},{17,25},{25,1},{2,10},{10... | collective-permute-start | bytes 970760 | tf_op jit(solution)/shard_map/ppermute | solution.py:243
  51.8 34.8 %copy-start.5 = (f32[8,10112]{1,0:T(8,128)S(1)}, f32[8,10112]{1,0:T(8,128)}, u32[]{:S(2)}) copy-start(f32[8,10112]{1,0:T(8,128)} %get-tuple-element.59.refs_6_) | copy-start | bytes 970756
  51.8 34.8 %collective-permute-start.9 = (f32[8,10112]{1,0:T(8,128)}, f32[8,10112]{1,0:T(8,128)S(1)}, u32[]{:S(2)}, u32[]{:S(2)}) collective-permute-start(f32[8,10112]{1,0:T(8,128)} %get-tuple-element.61), channel_id=1, source_target_pairs={{0,16},{8,24},{16,0},{24,8},{1,17},{9,25},{17,1},{25,9},{2,18},{10... | collective-permute-start | bytes 970760 | tf_op jit(solution)/shard_map/ppermute | solution.py:243
  57.1 23.0 %collective-permute-start.6 = (f32[8,128]{1,0:T(8,128)S(1)}, f32[8,128]{1,0:T(8,128)S(1)}, u32[]{:S(2)}, u32[]{:S(2)}) collective-permute-start(f32[8,128]{1,0:T(8,128)S(1)} %bitcast_reduce_fusion.refs_7_), channel_id=1, source_target_pairs={{0,16},{8,24},{16,0},{24,8},{1,17},{9,25},{17,1},{25,9},{2,18},{10... | collective-permute-start | bytes 12296 | tf_op jit(solution)/shard_map/ppermute | solution.py:243
  57.2 24.8 %collective-permute-start.7 = (f32[8,128]{1,0:T(8,128)S(1)}, f32[8,128]{1,0:T(8,128)S(1)}, u32[]{:S(2)}, u32[]{:S(2)}) collective-permute-start(f32[8,128]{1,0:T(8,128)S(1)} %bitcast_reduce_fusion.refs_7_), channel_id=1, source_target_pairs={{0,24},{8,0},{16,8},{24,16},{1,25},{9,1},{17,9},{25,17},{2,26},{10... | collective-permute-start | bytes 12296 | tf_op jit(solution)/shard_map/ppermute | solution.py:243
  80.1 15.5 %collective-permute-start.16 = (f32[4,2,8,896]{3,2,1,0:T(8,128)S(1)}, f32[4,2,8,896]{3,2,1,0:T(8,128)S(1)}, u32[]{:S(2)}, u32[]{:S(2)}) collective-permute-start(f32[4,2,8,896]{3,2,1,0:T(8,128)S(1)} %get-tuple-element.70), channel_id=1, source_target_pairs={{0,1},{1,2},{2,3},{3,4},{4,5},{5,6},{6,7},{8,9},{9,10},{10,11},{11... | collective-permute-start | bytes 688136 | tf_op jit(solution)/shard_map/ppermute | solution.py:408
  82.0 13.5 %collective-permute-start.17 = (f32[4,2,8,896]{3,2,1,0:T(8,128)S(1)}, f32[4,2,8,896]{3,2,1,0:T(8,128)S(1)}, u32[]{:S(2)}, u32[]{:S(2)}) collective-permute-start(f32[4,2,8,896]{3,2,1,0:T(8,128)S(1)} %get-tuple-element.71), channel_id=1, source_target_pairs={{1,0},{2,1},{3,2},{4,3},{5,4},{6,5},{7,6},{9,8},{10,9},{11,10},{12... | collective-permute-start | bytes 688136 | tf_op jit(solution)/shard_map/ppermute | solution.py:409
  90.2 27.2 %collective-permute-start.13 = (f32[8,10112]{1,0:T(8,128)}, f32[8,10112]{1,0:T(8,128)S(1)}, u32[]{:S(2)}, u32[]{:S(2)}) collective-permute-start(f32[8,10112]{1,0:T(8,128)} %get-tuple-element.67), channel_id=1, source_target_pairs={{0,8},{8,16},{16,24},{24,0},{1,9},{9,17},{17,25},{25,1},{2,10},{10... | collective-permute-start | bytes 970760 | tf_op jit(solution)/shard_map/ppermute | solution.py:243
  90.6 28.0 %collective-permute-start.14 = (f32[8,10112]{1,0:T(8,128)}, f32[8,10112]{1,0:T(8,128)S(1)}, u32[]{:S(2)}, u32[]{:S(2)}) collective-permute-start(f32[8,10112]{1,0:T(8,128)} %get-tuple-element.68), channel_id=1, source_target_pairs={{0,16},{8,24},{16,0},{24,8},{1,17},{9,25},{17,1},{25,9},{2,18},{10... | collective-permute-start | bytes 970760 | tf_op jit(solution)/shard_map/ppermute | solution.py:243
  94.7 27.7 %collective-permute-start.15 = (f32[8,10112]{1,0:T(8,128)}, f32[8,10112]{1,0:T(8,128)S(1)}, u32[]{:S(2)}, u32[]{:S(2)}) collective-permute-start(f32[8,10112]{1,0:T(8,128)} %get-tuple-element.69), channel_id=1, source_target_pairs={{0,24},{8,0},{16,8},{24,16},{1,25},{9,1},{17,9},{25,17},{2,26},{10... | collective-permute-start | bytes 970760 | tf_op jit(solution)/shard_map/ppermute | solution.py:243
  95.5 1.0 copy-start.3
  101.6 9.1 %collective-permute-start.18 = (f32[4,2,8,896]{3,2,1,0:T(8,128)S(1)}, f32[4,2,8,896]{3,2,1,0:T(8,128)S(1)}, u32[]{:S(2)}, u32[]{:S(2)}) collective-permute-start(f32[4,2,8,896]{3,2,1,0:T(8,128)S(1)} %get-tuple-element.73), channel_id=1, source_target_pairs={{0,1},{1,2},{2,3},{3,4},{4,5},{5,6},{6,7},{8,9},{9,10},{10,11},{11... | collective-permute-start | bytes 688136 | tf_op jit(solution)/shard_map/ppermute | solution.py:408
  103.5 8.1 %collective-permute-start.19 = (f32[4,2,8,896]{3,2,1,0:T(8,128)S(1)}, f32[4,2,8,896]{3,2,1,0:T(8,128)S(1)}, u32[]{:S(2)}, u32[]{:S(2)}) collective-permute-start(f32[4,2,8,896]{3,2,1,0:T(8,128)S(1)} %get-tuple-element.74), channel_id=1, source_target_pairs={{1,0},{2,1},{3,2},{4,3},{5,4},{6,5},{7,6},{9,8},{10,9},{11,10},{12... | collective-permute-start | bytes 688136 | tf_op jit(solution)/shard_map/ppermute | solution.py:409
  117.4 5.4 %copy-start.1 = (f32[25,2,8,800]{3,1,0,2:T(2,128)}, f32[25,2,8,800]{3,1,0,2:T(2,128)S(1)}, u32[]{:S(2)}) copy-start(f32[25,2,8,800]{3,1,0,2:T(2,128)S(1)} %copy.28) | copy-start | bytes 3840004
where the time goes:
time: 125 us
  starting transfers between devices  44.4 us (36%)
  Pallas kernels  32 us (26%)
  waiting for transfers between devices  23.2 us (19%)
  local copies, waits for them, and re-layouts  16.7 us (13%)
  blocking collectives  7.28 us (6%)
    pallas_call x11, Pallas kernels, call(): pl.pallas_call(ordered, out_shape=out_shape, in_specs=in_specs + [ANY] *...  32 us
    ppermute x12, waiting for transfers between devices, exchange(): lax.ppermute(parts[shift], 'member', [(i, (i + shift) % members) for i in...  22.2 us
    ppermute x12, starting transfers between devices, exchange(): lax.ppermute(parts[shift], 'member', [(i, (i + shift) % members) for i in...  18.3 us
    ppermute x4, starting transfers between devices, step(): right = lax.ppermute(head, 'space', [(i + 1, i) for i in range(spaces - 1)])  18.2 us
    unnamed x25, local copies, waits for them, and re-layouts  9.13 us
    ppermute x4, starting transfers between devices, step(): left = lax.ppermute(tail, 'space', [(i, i + 1) for i in range(spaces - 1)])  7.92 us
    all_gather x1, blocking collectives, shards(): dist = jnp.sum(lax.all_gather(dist, 'space', axis=0), axis=0)  7.28 us
    optimization_barrier x2, local copies, waits for them, and re-layouts, shards(): lax.optimization_barrier((ready, loglik_grad, wave_prev, wave_now, ghosts...  3.57 us
  transfers between devices with their start and end apart: 20, of which 5 were waited for; matrix products, arithmetic and copies ran while one was open for 7% of the time, Pallas kernels for 25%

commit v1 on v0

v1 whole, which is shorter than its diff:
```python
import functools
import math

import jax
import jax.numpy as jnp
from jax import lax
from jax.experimental import pallas as pl
from jax.experimental.pallas import tpu as pltpu
from jax.sharding import PartitionSpec as P


GHOST = 4
STEPS = 4
LANES = 128

weights = (-205.0 / 72.0, 8.0 / 5.0, -1.0 / 5.0, 8.0 / 315.0, -1.0 / 560.0)
step_size = 0.25
courant = 0.3

VMEM = pl.BlockSpec(memory_space=pltpu.VMEM)
SMEM = pl.BlockSpec(memory_space=pltpu.SMEM)


ANY = pl.BlockSpec(memory_space=pl.ANY)
HBM = pl.BlockSpec(memory_space=pltpu.HBM)


def held(shape, space=pltpu.VMEM):
    return space(tuple(shape), jnp.float32)


def blocks_of(width):
    size = -(-width // 5)
    return [(low, min(low + size, width)) for low in range(0, width, size)]


def call(body, out_shape, in_specs, out_specs, operands, scratch_shapes=(), after=(), near=(), away=()):
    n_in, n_after = len(operands), len(after)
    in_specs, out_specs, operands = list(in_specs), list(out_specs), list(operands)
    scratch = list(scratch_shapes)
    moves = [(i, operands[i]) for i in near] + [(n_in + i, out_shape[i]) for i in away]
    for i, _ in moves:
        if i < n_in:
            in_specs[i] = HBM
            operands[i] = pltpu.with_memory_space_constraint(operands[i], pltpu.HBM)
        else:
            out_specs[i - n_in] = HBM
    if moves:
        blocks = blocks_of(moves[0][1].shape[1])
        scratch += [pltpu.VMEM(array.shape, jnp.float32) for _, array in moves]
        scratch += [pltpu.SemaphoreType.DMA((len(moves), len(blocks)))]

    def ordered(*refs):
        refs = list(refs[:n_in] + refs[n_in + n_after :])
        if not moves:
            return body(*refs)
        refs, stages, sems = refs[: -len(moves) - 1], refs[-len(moves) - 1 : -1], refs[-1]
        coming, leaving = [], []
        for k, (low, high) in enumerate(blocks):
            coming.append([])
            leaving.append([])
            for m, (i, _) in enumerate(moves):
                home, here = refs[i].at[:, low:high], stages[m].at[:, low:high]
                if i < n_in:
                    coming[k].append(pltpu.make_async_copy(home, here, sems.at[m, k]))
                    coming[k][-1].start()
                else:
                    leaving[k].append(pltpu.make_async_copy(here, home, sems.at[m, k]))
        for m, (i, _) in enumerate(moves):
            refs[i] = stages[m]

        def arrive(k):
            for copy in coming[k]:
                copy.wait()

        def leave(k):
            for copy in leaving[k]:
                copy.start()

        body(*refs, arrive=arrive, leave=leave)
        for copies in leaving:
            for copy in copies:
                copy.wait()

    return pl.pallas_call(
        ordered,
        out_shape=out_shape,
        in_specs=in_specs + [ANY] * n_after,
        out_specs=out_specs,
        scratch_shapes=scratch,
        compiler_params=pltpu.CompilerParams(vmem_limit_bytes=26 << 20),
    )(*operands, *after)


class Packing:
    def __init__(self, width, depth, across, members):
        self.width, self.depth, self.across, self.members = width, depth, across, members
        self.rows = width * depth
        self.full = across // LANES
        self.tail = across % LANES
        self.group = LANES // self.tail if self.tail else 1
        self.tail_tiles = -(-self.rows // self.group) if self.tail else 0
        total = self.rows * self.full + self.tail_tiles
        self.tiles = -(-total // members)
        self.lanes = self.tiles * LANES
        self.spare = self.tiles * members - total

    def runs(self, row):
        tile, at, left = row * self.full, 0, self.full
        while left:
            chunk, place = divmod(tile, self.tiles)
            count = min(left, self.tiles - place)
            yield chunk, place * LANES, at * LANES, count * LANES
            tile, at, left = tile + count, at + count, left - count

    def tail_place(self, index):
        chunk, place = divmod(self.rows * self.full + index, self.tiles)
        return chunk, place * LANES


def pack_body(pack, cuts, me_ref, cells_ref, *refs, arrive, leave):
    outs, buf = refs[:-1], refs[-1]
    own = cells_ref.shape[0]
    me = me_ref[0]
    slots = [lax.rem(chunk - me + pack.members, pack.members) for chunk in range(pack.members)]
    starts = {low: k for k, (low, _) in enumerate(blocks_of(pack.width))}
    for row in range(pack.rows):
        x, z = divmod(row, pack.depth)
        if z == 0 and x in starts:
            arrive(starts[x])
        for chunk, there, here, count in pack.runs(row):
            buf[slots[chunk], :, there : there + count] = cells_ref[:, x, z, here : here + count]
    start = pack.full * LANES
    for index in range(pack.tail_tiles):
        chunk, place = pack.tail_place(index)
        pieces = []
        for row in range(index * pack.group, min(pack.rows, (index + 1) * pack.group)):
            x, z = divmod(row, pack.depth)
            pieces.append(cells_ref[:, x, z, start : start + pack.tail])
        empty = LANES - pack.tail * len(pieces)
        if empty:
            pieces.append(jnp.zeros((own, empty), jnp.float32))
        buf[slots[chunk], :, place : place + LANES] = jnp.concatenate(pieces, axis=1)
    for index in range(pack.spare):
        chunk, place = pack.tail_place(pack.tail_tiles + index)
        buf[slots[chunk], :, place : place + LANES] = jnp.zeros((own, LANES), jnp.float32)
    at = 0
    for low, high in cuts:
        for slot in range(pack.members):
            outs[at][...] = buf[slot, :, low:high]
            at += 1


def packed(pack, cuts, me, cells, after=()):
    own = cells.shape[0]
    outs = call(
        functools.partial(pack_body, pack, cuts),
        out_shape=[
            held((own, high - low), pltpu.HBM)
            for low, high in cuts
            for _ in range(pack.members)
        ],
        in_specs=[SMEM, VMEM],
        out_specs=[VMEM] * (len(cuts) * pack.members),
        operands=[me, cells],
        near=(1,),
        scratch_shapes=[pltpu.VMEM((pack.members, own, pack.lanes), jnp.float32)],
        after=after,
    )
    return [outs[i * pack.members : (i + 1) * pack.members] for i in range(len(cuts))]


def unpack_body(pack, cuts, me_ref, *refs, arrive, leave):
    parts, out_ref, buf = refs[:-2], refs[-2], refs[-1]
    me = me_ref[0]
    at = 0
    for low, high in cuts:
        for shift in range(pack.members):
            chunk = lax.rem(me - shift + pack.members, pack.members)
            buf[chunk, :, low:high] = parts[at][...]
            at += 1
    start = pack.full * LANES
    for k, (low, high) in enumerate(blocks_of(pack.width)):
        for row in range(low * pack.depth, high * pack.depth):
            x, z = divmod(row, pack.depth)
            for chunk, there, here, count in pack.runs(row):
                out_ref[:, x, z, here : here + count] = buf[chunk, :, there : there + count]
            if pack.tail:
                chunk, place = pack.tail_place(row // pack.group)
                tile = buf[chunk, :, place : place + LANES]
                at = row % pack.group * pack.tail
                out_ref[:, x, z, start:] = tile[:, at : at + pack.tail]
        leave(k)


def unpacked(pack, cuts, me, parts, after=()):
    own = parts[0].shape[0]
    return call(
        functools.partial(unpack_body, pack, cuts),
        out_shape=[held((own, pack.width, pack.depth, pack.across), pltpu.HBM)],
        in_specs=[SMEM] + [VMEM] * len(parts),
        out_specs=[VMEM],
        operands=[me, *parts],
        scratch_shapes=[pltpu.VMEM((pack.members, own, pack.lanes), jnp.float32)],
        after=after,
        away=(0,),
    )


def distance_body(members, me_ref, *refs):
    parts, out_ref, all_ref = refs[:members], refs[members], refs[members + 1]
    own = parts[0].shape[0]
    me = me_ref[0]
    for shift in range(members):
        row = pl.multiple_of(lax.rem(me - shift + members, members) * own, own)
        all_ref[pl.ds(row, own), :] = parts[shift][...]
    cells = all_ref[...]
    cells = cells - cells[0:1, :]
    gram = lax.dot_general(
        cells,
        cells,
        (((1,), (1,)), ((), ())),
        precision=lax.Precision.HIGHEST,
        preferred_element_type=jnp.float32,
    )
    count = gram.shape[0]
    rows = lax.broadcasted_iota(jnp.int32, (count, count), 0)
    cols = lax.broadcasted_iota(jnp.int32, (count, count), 1)
    diag = jnp.where(rows == cols, gram, 0.0)
    down = jnp.sum(diag, axis=1, keepdims=True)
    along = jnp.sum(diag, axis=0, keepdims=True)
    dist = jnp.where(rows == cols, 0.0, down + along - 2.0 * gram)
    for member in range(members):
        out_ref[:, member * count : (member + 1) * count] = dist[member * own : (member + 1) * own]


def distances(members, me, parts, after=()):
    own, lanes = parts[0].shape
    count = own * members
    return call(
        functools.partial(distance_body, members),
        out_shape=[held((own, members * count))],
        in_specs=[SMEM] + [VMEM] * members,
        out_specs=[VMEM],
        operands=[me, *parts],
        scratch_shapes=[pltpu.VMEM((count, lanes), jnp.float32)],
        after=after,
    )


def add_body(*refs):
    total = refs[0][...]
    for ref in refs[1:-1]:
        total = total + ref[...]
    refs[-1][...] = total


def added(arrays):
    return call(
        add_body, out_shape=[held(arrays[0].shape)], in_specs=[VMEM] * len(arrays), out_specs=[VMEM], operands=arrays
    )


def update_body(members, low, me_ref, dist_ref, *refs):
    cells, grads = refs[:members], refs[members : 2 * members]
    outs = refs[2 * members : 3 * members]
    cell_ref, grad_ref, out_ref = refs[3 * members :]
    own, lanes = grads[0].shape
    count = own * members
    me = me_ref[0]
    for shift in range(members):
        row = pl.multiple_of(lax.rem(me - shift + members, members) * own, own)
        cell_ref[pl.ds(row, own), :] = cells[shift][:, low : low + lanes]
        grad_ref[pl.ds(row, own), :] = grads[shift][...]
    parts = dist_ref[0]
    for index in range(1, dist_ref.shape[0]):
        parts = parts + dist_ref[index]
    dist = jnp.concatenate(
        [parts[:, member * count : (member + 1) * count] for member in range(members)], axis=0
    )
    band = jnp.sum(jnp.sum(dist, axis=1, keepdims=True), axis=0, keepdims=True) / (
        count * (count - 1) * math.log(count + 1)
    )
    kern = jnp.exp(-dist / band)
    total = jnp.sum(kern, axis=1, keepdims=True)
    cell = cell_ref[...]
    mixed = 0.5 * band * grad_ref[...] - cell
    pulled = jnp.dot(
        kern, mixed, precision=lax.Precision.HIGHEST, preferred_element_type=jnp.float32
    )
    out_ref[...] = cell + step_size * (pulled + total * cell)
    for shift in range(members):
        row = pl.multiple_of(lax.rem(me + shift, members) * own, own)
        outs[shift][...] = out_ref[pl.ds(row, own), :]


def updated(members, low, me, dist, cells, grads, after=()):
    own, lanes = grads[0].shape
    count = own * members
    return call(
        functools.partial(update_body, members, low),
        out_shape=[held((own, lanes), pltpu.HBM)] * members,
        in_specs=[SMEM, VMEM] + [VMEM] * (2 * members),
        out_specs=[VMEM] * members,
        operands=[me, dist, *cells, *grads],
        scratch_shapes=[pltpu.VMEM((count, lanes), jnp.float32)] * 3,
        after=after,
    )


def exchange(parts, members):
    return [parts[0]] + [
        lax.ppermute(parts[shift], "member", [(i, (i + shift) % members) for i in range(members)])
        for shift in range(1, members)
    ]


def edges_of(side_ref, cells_ref, inner, outer):
    width, count = cells_ref.shape[0], inner.shape[0]
    side = side_ref[0]
    inner[...] = cells_ref[pl.ds((width - count) * (1 - side), count)]
    outer[...] = cells_ref[pl.ds((width - count) * side, count)]


def between(side_ref, wide, inner_ref, cells_ref, outer_ref):
    width, depth, own, across = cells_ref.shape
    count, lanes = inner_ref.shape[0], wide.shape[-1]
    side = side_ref[0]
    start = (across // LANES) * LANES
    places = ((count + width) * (1 - side), inner_ref), (count, cells_ref), ((count + width) * side, outer_ref)
    for first, part in places:

        def fill(x, carry, first=first, part=part):
            for z in range(depth):
                if lanes > across:
                    wide[first + x, z, :, start:] = jnp.zeros((own, lanes - start), jnp.float32)
                wide[first + x, z, :, :across] = part[x, z]
            return carry

        lax.fori_loop(0, part.shape[0], fill, 0)


def hold_body(side_ref, cells_ref, out_ref, inner_ref, outer_ref, arrive, leave):
    width, depth = out_ref.shape[:2]

    def one(x, carry):
        for z in range(depth):
            out_ref[x, z] = cells_ref[:, x, z, :]
        return carry

    for k, (low, high) in enumerate(blocks_of(width)):
        arrive(k)
        lax.fori_loop(low, high, one, 0)
    edges_of(side_ref, out_ref, inner_ref, outer_ref)


def hold(side, cells, after=()):
    own, width, depth, across = cells.shape
    edge = held((GHOST, depth, own, across))
    return call(
        hold_body,
        out_shape=[held((width, depth, own, across)), edge, edge],
        in_specs=[SMEM, VMEM],
        out_specs=[VMEM] * 3,
        operands=[side, cells],
        near=(1,),
        after=after,
    )


def medium_body(side_ref, cells_ref, ghosts_ref, prev_ref, coef_ref, still_ref, out_ref, inner_ref, outer_ref, arrive, leave):
    own, width, depth, across = cells_ref.shape

    def one(x, carry):
        for z in range(depth):
            out_ref[x, z] = prev_ref[:, x, z, :]
            speed = courant * (1.0 + 0.3 * jnp.tanh(cells_ref[:, x, z, :]))
            coef_ref[x, z] = speed * speed
            total = None
            for offset in range(1, GHOST + 1):
                terms = []
                if z - offset < 0:
                    terms.append(ghosts_ref[:, x, GHOST + z - offset, :])
                if z + offset >= depth:
                    terms.append(ghosts_ref[:, x, GHOST + z + offset - depth, :])
                for term in terms:
                    part = weights[offset] * term
                    total = part if total is None else total + part
            still_ref[x, z] = jnp.zeros((own, across), jnp.float32) if total is None else total
        return carry

    for k, (low, high) in enumerate(blocks_of(width)):
        arrive(k)
        lax.fori_loop(low, high, one, 0)
    for k, ref in enumerate((coef_ref, still_ref)):
        rows = slice(k * GHOST, (k + 1) * GHOST)
        edges_of(side_ref, ref, inner_ref.at[rows], outer_ref.at[rows])


def medium(side, cells, ghosts, prev, after=()):
    own, width, depth, across = cells.shape
    edge = held((2 * GHOST, depth, own, across))
    return call(
        medium_body,
        out_shape=[held((width, depth, own, across))] * 3 + [edge] * 2,
        in_specs=[SMEM] + [VMEM] * 3,
        out_specs=[VMEM] * 5,
        operands=[side, cells, ghosts, prev],
        near=(1, 2, 3),
        after=after,
    )


def sweep(amplitude, across, rows, first, place_ref, source_ref, wide, sums, prev, coef, still, store):
    depth, own, lanes = wide.shape[1:]
    tiles = lanes // LANES
    lane = lax.broadcasted_iota(jnp.int32, (own, LANES), 1)
    particle = lax.broadcasted_iota(jnp.int32, (own, LANES), 0)
    spot = -lane
    for index in range(own):
        cell = source_ref[index] - place_ref[1] * across
        spot = spot + jnp.where(particle == index, cell, 0)

    def tile(t):
        return slice(t * LANES, (t + 1) * LANES)

    def moved(row, t, by):
        up = jnp.where(lane >= by, pltpu.roll(row[t], by, 1), pltpu.roll(row[t - 1], by, 1))
        here, after = row[t], row[(t + 1) % tiles]
        down = jnp.where(
            lane < LANES - by, pltpu.roll(here, LANES - by, 1), pltpu.roll(after, LANES - by, 1)
        )
        return up, down

    def blend(x):
        for z in range(depth):
            row = [wide[x + GHOST, z, :, tile(t)] for t in range(tiles)]
            for t in range(tiles):
                up, down = moved(row, t, 1)
                near, slope = up + down, up - down
                even = (0.5 * (weights[2] + weights[4])) * near + weights[3] * row[t]
                odd = (0.5 * (weights[2] - weights[4])) * slope
                sums[0, x, z, :, tile(t)] = weights[1] * near + (3.0 * weights[0]) * row[t]
                sums[1, x, z, :, tile(t)] = even - odd
                sums[2, x, z, :, tile(t)] = even + odd

    def advance(x):
        for z in range(depth):
            plus = [sums[1, x, z, :, tile(t)] for t in range(tiles)]
            minus = [sums[2, x, z, :, tile(t)] for t in range(tiles)]
            for t in range(tiles):
                count = min(LANES, across - t * LANES)
                if count <= 0:
                    continue
                here = tile(t)
                total = sums[0, x, z, :, here]
                for offset in range(1, GHOST + 1):
                    pair = wide[x + GHOST + offset, z, :, here] + wide[x + GHOST - offset, z, :, here]
                    if z - offset >= 0:
                        pair = pair + wide[x + GHOST, z - offset, :, here]
                    if z + offset < depth:
                        pair = pair + wide[x + GHOST, z + offset, :, here]
                    total = total + weights[offset] * pair
                total = total + (moved(plus, t, 3)[0] + moved(minus, t, 3)[1])
                center, total = wide[x + GHOST, z, :, here][:, :count], total[:, :count]
                there = slice(t * LANES, t * LANES + count)
                total = total + still[x, z, :, there]
                value = 2.0 * center - prev[x, z, :, there] + coef[x, z, :, there] * total
                if z == 0:
                    hit = (spot == (x + first) * across + t * LANES)[:, :count]
                    value = value + jnp.where(hit, amplitude, 0.0)
                store(x, z, there, value)

    def one(x, carry):
        advance(x - 1)
        blend(x)
        return carry

    blend(0)
    lax.fori_loop(1, rows, one, 0)
    advance(rows - 1)


def wave_body(
    amplitude, side_ref, source_ref, inner_ref, outer_ref, now_ref, prev_ref, coef_ref, still_ref,
    out_ref, to_inner_ref, to_outer_ref, wide, sums,
):
    width, _, _, across = now_ref.shape

    def store(x, z, there, value):
        out_ref[x, z, :, there] = value

    between(side_ref, wide, inner_ref, now_ref, outer_ref)
    sweep(amplitude, across, width, 0, side_ref, source_ref, wide, sums, prev_ref, coef_ref, still_ref, store)
    edges_of(side_ref, out_ref, to_inner_ref, to_outer_ref)


def lanes_of(across):
    return -(-(across + GHOST) // LANES) * LANES


def wave_step(amplitude, reach, side, source, edges, now, prev, coef, still, after=()):
    width, depth, own, across = now.shape
    lanes = lanes_of(across)
    return call(
        functools.partial(wave_body, amplitude),
        out_shape=[held(now.shape)] + [held((reach,) + now.shape[1:])] * 2,
        in_specs=[SMEM] * 2 + [VMEM] * 6,
        out_specs=[VMEM] * 3,
        operands=[side, source, *edges, now, prev, coef, still],
        scratch_shapes=[
            pltpu.VMEM((width + 2 * GHOST, depth, own, lanes), jnp.float32),
            pltpu.VMEM((3, width, depth, own, lanes), jnp.float32),
        ],
        after=after,
    )


def last_body(
    amplitudes, side_ref, source_ref, inner_ref, outer_ref, now_ref, before_inner, before_outer, prev_ref,
    medium_inner, medium_outer, coef_ref, still_ref, token_ref, first_ref, second_ref,
    wide, middle, prev, coef, still, sums,
):
    width, depth, own, across = now_ref.shape
    lanes = wide.shape[-1]
    start = (across // LANES) * LANES
    token_ref[...] = jnp.zeros(token_ref.shape, jnp.float32)
    between(side_ref, wide, inner_ref, now_ref, outer_ref)
    between(side_ref, prev, before_inner, prev_ref, before_outer)
    halves = [slice(0, GHOST), slice(GHOST, 2 * GHOST)]
    between(side_ref, coef, medium_inner.at[halves[0]], coef_ref, medium_outer.at[halves[0]])
    between(side_ref, still, medium_inner.at[halves[1]], still_ref, medium_outer.at[halves[1]])

    def clear(x, carry):
        for z in range(depth):
            middle[x, z, :, start:] = jnp.zeros((own, lanes - start), jnp.float32)
        return carry

    lax.fori_loop(0, width + 2 * GHOST, clear, 0)

    def keep(x, z, there, value):
        middle[x, z, :, there] = value

    sweep(amplitudes[0], across, width + 2 * GHOST, -GHOST, side_ref, source_ref, wide, sums, prev, coef, still, keep)

    def turn(x, carry):
        for z in range(depth):
            first_ref[:, x, z, :] = middle[x + GHOST, z, :, :across]
        return carry

    lax.fori_loop(0, width, turn, 0)

    def store(x, z, there, value):
        second_ref[:, x, z, there] = value

    own_rows = wide.at[2 * GHOST : 2 * GHOST + width]
    sweep(amplitudes[1], across, width, 0, side_ref, source_ref, middle, sums, own_rows, coef_ref, still_ref, store)


def last_steps(amplitudes, side, source, edges, now, before, prev, around, coef, still, after=()):
    width, depth, own, across = now.shape
    lanes = lanes_of(across)
    extended = pltpu.VMEM((width + 2 * GHOST, depth, own, lanes), jnp.float32)
    native = held((own, width, depth, across), pltpu.HBM)
    return call(
        functools.partial(last_body, amplitudes),
        out_shape=[held((own, LANES)), native, native],
        in_specs=[SMEM] * 2 + [VMEM] * 10,
        out_specs=[VMEM] * 3,
        operands=[side, source, *edges, now, *before, prev, *around, coef, still],
        scratch_shapes=[
            pltpu.VMEM((width + 4 * GHOST, depth, own, lanes), jnp.float32),
            extended,
            extended,
            extended,
            extended,
            pltpu.VMEM((3, width + 2 * GHOST, depth, own, lanes), jnp.float32),
        ],
        after=after,
    )


def shards(cuts_of, particles, loglik_grad, wave_prev, wave_now, ghosts, src_cell):
    _, depth, width, across = particles.shape
    members = lax.axis_size("member")
    spaces = lax.axis_size("space")
    member_idx = lax.axis_index("member")
    space_idx = lax.axis_index("space")
    pack = Packing(width, depth, across, members)
    whole = [(0, pack.lanes)]
    cuts = cuts_of(pack)
    me = jnp.reshape(member_idx, (1,)).astype(jnp.int32)

    def turned(array):
        return jnp.transpose(array, (0, 2, 1, 3))

    ready = packed(pack, whole, me, turned(particles))[0]
    ready, wave_now = lax.optimization_barrier((ready, wave_now))
    cell_parts = exchange(ready, members)

    side = jnp.stack([space_idx % 2, space_idx * width]).astype(jnp.int32)
    now, inner, outer = hold(side, turned(wave_now))
    coef, still, prev, *around = medium(side, turned(particles), turned(ghosts), turned(wave_prev), after=[now])

    def swap(edge, first):
        pairs = [(i, i + 1) for i in range(first, spaces - 1, 2)]
        return lax.ppermute(edge, "space", pairs + [(j, i) for i, j in pairs])

    def swapped(inner, outer):
        return swap(inner, 0), swap(outer, 1)

    amplitudes = [2.0 * math.cos(1.3 * index) for index in range(STEPS)]
    waves = [prev, now]
    edges = swapped(inner, outer)
    around = swapped(*around)

    def step(index, edges, after=()):
        reach = GHOST if index < STEPS - 3 else 2 * GHOST
        out, inner, outer = wave_step(
            amplitudes[index], reach, side, src_cell, edges, waves[-1], waves[-2], coef, still, after=after
        )
        waves.append(out)
        return swapped(inner, outer)

    before, edges = edges, step(0, edges)
    grads = packed(pack, cuts, me, turned(loglik_grad), after=[waves[-1]])
    grad_parts = []
    for part in grads:
        grad_parts.append(exchange(part, members))
    dist = distances(members, me, cell_parts, after=[waves[2]])[0]
    dist = exchange([dist] * members, members)
    dist = added(dist)[0]
    dist = lax.all_gather(dist, "space", axis=0)
    for index in range(1, STEPS - 2):
        before, edges = edges, step(index, edges, after=[dist])

    moved = []
    order = dist
    for (low, _), grads in zip(cuts, grad_parts):
        out = updated(members, low, me, dist, cell_parts, grads, after=[order])
        order = out[0]
        moved += exchange(out, members)
    token, *ends = last_steps(
        amplitudes[-2:], side, src_cell, edges, waves[-1], before, waves[-2], around, coef, still, after=[order]
    )
    new_particles = unpacked(pack, cuts, me, moved, after=[token])[0]
    return turned(new_particles), turned(ends[0]), turned(ends[1])


def early_cut(pack):
    first = pack.tiles * 1 // 4 * LANES
    return [(0, first), (first, pack.lanes)]


def solution(mesh):
    spec = P("member", None, "space", None)
    return jax.shard_map(
        functools.partial(shards, early_cut),
        mesh=mesh,
        in_specs=(spec, spec, spec, spec, spec, P("member")),
        out_specs=(spec, spec, spec),
        check_vma=False,
    )
```

time: 125 us -> 141 us (1.13)
  the two profiles are of different devices: /device:TPU:12 before, /device:TPU:0 now
where the time goes in v1:
time: 141 us; the launch traced here: 139 us
  starting transfers between devices  42.2 us (30%)
  Pallas kernels  39 us (28%)
  waiting for transfers between devices  34.1 us (24%)
  blocking collectives  20.6 us (15%)
  local copies, waits for them, and re-layouts  1.88 us (1%)
    pallas_call x12, Pallas kernels, call(): pl.pallas_call(ordered, out_shape=out_shape, in_specs=in_specs + [ANY] *...  39 us
    ppermute x18, starting transfers between devices, exchange(): lax.ppermute(parts[shift], 'member', [(i, (i + shift) % members) for i in...  34.9 us
    ppermute x18, waiting for transfers between devices, exchange(): lax.ppermute(parts[shift], 'member', [(i, (i + shift) % members) for i in...  34.1 us
    all_gather x1, blocking collectives, shards(): dist = lax.all_gather(dist, 'space', axis=0)  20.6 us
    ppermute x8, starting transfers between devices, swap(): return lax.ppermute(edge, 'space', pairs + [(j, i) for i, j in pairs])  7.32 us
  transfers between devices with their start and end apart: 26, of which 7 were waited for; matrix products, arithmetic and copies ran while one was open for 0% of the time, Pallas kernels for 24%

profile of v1, /device:TPU:0, one launch (start us, length us, event | category | flops | bytes accessed | tf_op | source)
XLA Modules:
  0.0 138.7 jit_solution(8912754275778929336)
XLA Ops:
  0.6 2.7 %shard_map.85 = (f32[8,10112]{1,0:T(8,128)}, f32[8,10112]{1,0:T(8,128)}, f32[8,10112]{1,0:T(8,128)}, f32[8,10112]{1,0:T(8,128)}) custom-call(s32[1]{0:T(128)} %bitcast.refs_0_, f32[8,25,2,800]{3,2,1,0:T(2,128)} %bitcast.17), custom_call_target="tpu_custom_call" | custom-call | tf_op jit(solution)/shard_map/pallas_call | solution.py:85
  3.5 2.0 %shard_map.86 = (f32[25,2,8,800]{3,2,1,0:T(8,128)S(1)}, f32[4,2,8,800]{3,2,1,0:T(8,128)S(1)}, f32[4,2,8,800]{3,2,1,0:T(8,128)S(1)}) custom-call(s32[2]{0:T(128)S(1)} %pad_add_fusion.refs_0_, f32[8,25,2,800]{3,2,1,0:T(2,128)} %bitcast.19), custom_call_target="tpu_custom_call" | custom-call | tf_op jit(solution)/shard_map/pallas_call | solution.py:85
  6.7 2.6 %collective-permute-start = (f32[8,10112]{1,0:T(8,128)S(1)}, f32[8,10112]{1,0:T(8,128)S(1)}, u32[]{:S(2)}, u32[]{:S(2)}) collective-permute-start(f32[8,10112]{1,0:T(8,128)S(1)} %copy-done.8), channel_id=1, source_target_pairs={{0,8},{8,16},{16,24},{24,0},{1,9},{9,17},{17,25},{25,1},{2,10},{10... | collective-permute-start | bytes 970760 | tf_op jit(solution)/shard_map/ppermute | solution.py:313
  9.4 2.6 %collective-permute-start.1 = (f32[8,10112]{1,0:T(8,128)S(1)}, f32[8,10112]{1,0:T(8,128)S(1)}, u32[]{:S(2)}, u32[]{:S(2)}) collective-permute-start(f32[8,10112]{1,0:T(8,128)S(1)} %copy-done.7), channel_id=1, source_target_pairs={{0,16},{8,24},{16,0},{24,8},{1,17},{9,25},{17,1},{25,9},{2,18},{10... | collective-permute-start | bytes 970760 | tf_op jit(solution)/shard_map/ppermute | solution.py:313
  12.0 1.3 collective-permute-start.2
  13.3 4.9 %shard_map.87 = (f32[25,2,8,800]{3,2,1,0:T(8,128)S(1)}, f32[25,2,8,800]{3,2,1,0:T(8,128)S(1)}, f32[25,2,8,800]{3,2,1,0:T(8,128)S(1)}, f32[8,2,8,800]{3,2,1,0:T(8,128)S(1)}, f32[8,2,8,800]{3,2,1,0:T(8,128)S(1)}) custom-call(s32[2]{0:T(128)S(1)} %pad_add_fusion.refs_0_, f32[8,25,2,800]{3,2,1,0:T(2,128)} %bitcast.18, f32[8,25,8,800]{3,2,1,0:T(8,128)} %bitcast.16, ...), custom_call_target="tpu_custom_call" | custom-call | tf_op jit(solution)/shard_map/pallas_call | solution.py:85
  18.3 4.3 %shard_map.88 = (f32[25,2,8,800]{3,2,1,0:T(8,128)S(1)}, f32[4,2,8,800]{3,2,1,0:T(8,128)S(1)}, f32[4,2,8,800]{3,2,1,0:T(8,128)S(1)}) custom-call(s32[2]{0:T(128)S(1)} %pad_add_fusion.refs_0_, s32[8]{0:T(128)S(1)} %copy-done.5, f32[4,2,8,800]{3,2,1,0:T(8,128)S(1)} %collective-permute-done.3.refs_2_, f32[4,2,8,800]{3,2,1,0:T(8,128)S(1)} %collective-permute-done.4.refs_3_, ...), custom_call_target="tpu_custom_call" | custom-call | tf_op jit(solution)/shard_map/pallas_call | solution.py:85
  22.5 2.7 %shard_map.91 = (f32[8,2432]{1,0:T(8,128)}, f32[8,2432]{1,0:T(8,128)}, f32[8,2432]{1,0:T(8,128)}, f32[8,2432]{1,0:T(8,128)}, f32[8,7680]{1,0:T(8,128)}, /*index=...) custom-call(s32[1]{0:T(128)} %bitcast.refs_0_, f32[8,25,2,800]{3,2,1,0:T(2,128)} %bitcast.20, ...), custom_call_target="tpu_custom_call" | custom-call | tf_op jit(solution)/shard_map/pallas_call | solution.py:85
  26.0 1.7 %collective-permute-start.20 = (f32[4,2,8,800]{3,2,1,0:T(8,128)S(1)}, f32[4,2,8,800]{3,2,1,0:T(8,128)S(1)}, u32[]{:S(2)}, u32[]{:S(2)}) collective-permute-start(f32[4,2,8,800]{3,2,1,0:T(8,128)S(1)} %get-tuple-element.77), channel_id=1, source_target_pairs={{0,1},{2,3},{4,5},{6,7},{1,0},{3,2},{5,4},{7,6},{8,9},{10,11},{12,... | collective-permute-start | bytes 614408 | tf_op jit(solution)/shard_map/ppermute | solution.py:607
  27.7 5.6 %collective-permute-done.8.refs_7_ = f32[8,2432]{1,0:T(8,128)S(1)} collective-permute-done((f32[8,2432]{1,0:T(8,128)}, f32[8,2432]{1,0:T(8,128)S(1)}, u32[]{:S(2)}, u32[]{:S(2)}) %collective-permute-start.8) | collective-permute-done | bytes 77856 | tf_op jit(solution)/shard_map/ppermute | solution.py:313
  33.3 8.2 %collective-permute-start.9 = (f32[8,2432]{1,0:T(8,128)}, f32[8,2432]{1,0:T(8,128)S(1)}, u32[]{:S(2)}, u32[]{:S(2)}) collective-permute-start(f32[8,2432]{1,0:T(8,128)} %get-tuple-element.63), channel_id=1, source_target_pairs={{0,16},{8,24},{16,0},{24,8},{1,17},{9,25},{17,1},{25,9},{2,18},{10... | collective-permute-start | bytes 233480 | tf_op jit(solution)/shard_map/ppermute | solution.py:313
  41.5 3.6 %collective-permute-done.9.refs_8_ = f32[8,2432]{1,0:T(8,128)S(1)} collective-permute-done((f32[8,2432]{1,0:T(8,128)}, f32[8,2432]{1,0:T(8,128)S(1)}, u32[]{:S(2)}, u32[]{:S(2)}) %collective-permute-start.9) | collective-permute-done | bytes 77856 | tf_op jit(solution)/shard_map/ppermute | solution.py:313
  45.9 2.0 %collective-permute-start.14 = (f32[8,7680]{1,0:T(8,128)}, f32[8,7680]{1,0:T(8,128)S(1)}, u32[]{:S(2)}, u32[]{:S(2)}) collective-permute-start(f32[8,7680]{1,0:T(8,128)} %get-tuple-element.70), channel_id=1, source_target_pairs={{0,8},{8,16},{16,24},{24,0},{1,9},{9,17},{17,25},{25,1},{2,10},{10... | collective-permute-start | bytes 737288 | tf_op jit(solution)/shard_map/ppermute | solution.py:313
  47.9 1.9 %collective-permute-start.15 = (f32[8,7680]{1,0:T(8,128)}, f32[8,7680]{1,0:T(8,128)S(1)}, u32[]{:S(2)}, u32[]{:S(2)}) collective-permute-start(f32[8,7680]{1,0:T(8,128)} %get-tuple-element.71), channel_id=1, source_target_pairs={{0,16},{8,24},{16,0},{24,8},{1,17},{9,25},{17,1},{25,9},{2,18},{10... | collective-permute-start | bytes 737288 | tf_op jit(solution)/shard_map/ppermute | solution.py:313
  49.8 1.3 shard_map.89.refs_0_
  51.7 5.5 %collective-permute-done.5.refs_1_ = f32[8,128]{1,0:T(8,128)S(1)} collective-permute-done((f32[8,128]{1,0:T(8,128)S(1)}, f32[8,128]{1,0:T(8,128)S(1)}, u32[]{:S(2)}, u32[]{:S(2)}) %collective-permute-start.5) | collective-permute-done | bytes 4128 | tf_op jit(solution)/shard_map/ppermute | solution.py:313
  57.2 4.7 %collective-permute-start.6 = (f32[8,128]{1,0:T(8,128)S(1)}, f32[8,128]{1,0:T(8,128)S(1)}, u32[]{:S(2)}, u32[]{:S(2)}) collective-permute-start(f32[8,128]{1,0:T(8,128)S(1)} %shard_map.89.refs_0_), channel_id=1, source_target_pairs={{0,16},{8,24},{16,0},{24,8},{1,17},{9,25},{17,1},{25,9},{2,18},{10... | collective-permute-start | bytes 12296 | tf_op jit(solution)/shard_map/ppermute | solution.py:313
  61.9 4.8 %collective-permute-done.6.refs_2_ = f32[8,128]{1,0:T(8,128)S(1)} collective-permute-done((f32[8,128]{1,0:T(8,128)S(1)}, f32[8,128]{1,0:T(8,128)S(1)}, u32[]{:S(2)}, u32[]{:S(2)}) %collective-permute-start.6) | collective-permute-done | bytes 4128 | tf_op jit(solution)/shard_map/ppermute | solution.py:313
  66.7 3.6 %collective-permute-done.7.refs_3_ = f32[8,128]{1,0:T(8,128)S(1)} collective-permute-done((f32[8,128]{1,0:T(8,128)S(1)}, f32[8,128]{1,0:T(8,128)S(1)}, u32[]{:S(2)}, u32[]{:S(2)}) %collective-permute-start.7) | collective-permute-done | bytes 4128 | tf_op jit(solution)/shard_map/ppermute | solution.py:313
  70.3 1.9 %collective-permute-start.24 = (f32[8,2,8,800]{3,2,1,0:T(8,128)S(1)}, f32[8,2,8,800]{3,2,1,0:T(8,128)S(1)}, u32[]{:S(2)}, u32[]{:S(2)}) collective-permute-start(f32[8,2,8,800]{3,2,1,0:T(8,128)S(1)} %get-tuple-element.82), channel_id=1, source_target_pairs={{0,1},{2,3},{4,5},{6,7},{1,0},{3,2},{5,4},{7,6},{8,9},{10,11},{12,... | collective-permute-start | bytes 1228808 | tf_op jit(solution)/shard_map/ppermute | solution.py:607
  72.9 2.1 %collective-permute-start.16 = (f32[8,7680]{1,0:T(8,128)S(1)}, f32[8,7680]{1,0:T(8,128)S(1)}, u32[]{:S(2)}, u32[]{:S(2)}) collective-permute-start(f32[8,7680]{1,0:T(8,128)S(1)} %copy-done.9), channel_id=1, source_target_pairs={{0,24},{8,0},{16,8},{24,16},{1,25},{9,1},{17,9},{25,17},{2,26},{10... | collective-permute-start | bytes 737288 | tf_op jit(solution)/shard_map/ppermute | solution.py:313
  75.1 20.6 %all-gather = f32[64,128]{1,0:T(8,128)S(1)} all-gather(f32[8,128]{1,0:T(8,128)S(1)} %shard_map.90), channel_id=2, replica_groups=mesh['member'=4,'space'=8] {'space'}, dimensions={0}, use_global_device_ids=true | all-gather | bytes 36864 | tf_op jit(solution)/shard_map/all_gather | solution.py:633
  95.7 4.3 %shard_map.94 = (f32[25,2,8,800]{3,2,1,0:T(8,128)S(1)}, f32[8,2,8,800]{3,2,1,0:T(8,128)S(1)}, f32[8,2,8,800]{3,2,1,0:T(8,128)S(1)}) custom-call(s32[2]{0:T(128)S(1)} %pad_add_fusion.refs_0_, s32[8]{0:T(128)S(1)} %copy-done.5, f32[4,2,8,800]{3,2,1,0:T(8,128)S(1)} %collective-permute-done.20.refs_2_.refs_5_, ...), custom_call_target="tpu_custom_call" | custom-call | tf_op jit(solution)/shard_map/pallas_call | solution.py:85
  101.1 1.3 shard_map.92
  102.4 1.3 collective-permute-start.11
  104.6 2.2 %shard_map.93 = (f32[8,7680]{1,0:T(8,128)}, f32[8,7680]{1,0:T(8,128)}, f32[8,7680]{1,0:T(8,128)}, f32[8,7680]{1,0:T(8,128)}) custom-call(s32[1]{0:T(128)} %bitcast.refs_0_, f32[8,8,128]{2,1,0:T(8,128)S(1)} %bitcast.15, f32[8,10112]{1,0:T(8,128)S(1)} %copy-done, f32[8,10112]{1,0:T(8,128)S(1)} %collective-permute-done.refs_2_.refs_3_, ...), custom_call_target="tpu_custom_call" | custom-call | tf_op jit(solution)/shard_map/pallas_call | solution.py:85
  106.7 2.1 %collective-permute-done.11.refs_2_ = f32[8,2432]{1,0:T(8,128)S(1)} collective-permute-done((f32[8,2432]{1,0:T(8,128)}, f32[8,2432]{1,0:T(8,128)S(1)}, u32[]{:S(2)}, u32[]{:S(2)}) %collective-permute-start.11) | collective-permute-done | bytes 77856 | tf_op jit(solution)/shard_map/ppermute | solution.py:313
  110.0 2.9 %collective-permute-start.19 = (f32[8,7680]{1,0:T(8,128)}, f32[8,7680]{1,0:T(8,128)S(1)}, u32[]{:S(2)}, u32[]{:S(2)}) collective-permute-start(f32[8,7680]{1,0:T(8,128)} %get-tuple-element.76), channel_id=1, source_target_pairs={{0,24},{8,0},{16,8},{24,16},{1,25},{9,1},{17,9},{25,17},{2,26},{10... | collective-permute-start | bytes 737288 | tf_op jit(solution)/shard_map/ppermute | solution.py:313
  112.9 1.8 %collective-permute-start.12 = (f32[8,2432]{1,0:T(8,128)S(1)}, f32[8,2432]{1,0:T(8,128)S(1)}, u32[]{:S(2)}, u32[]{:S(2)}) collective-permute-start(f32[8,2432]{1,0:T(8,128)S(1)} %copy-done.11), channel_id=1, source_target_pairs={{0,16},{8,24},{16,0},{24,8},{1,17},{9,25},{17,1},{25,9},{2,18},{10... | collective-permute-start | bytes 233480 | tf_op jit(solution)/shard_map/ppermute | solution.py:313
  116.6 11.9 %shard_map.95 = (f32[8,128]{1,0:T(8,128)S(1)}, f32[8,25,2,800]{3,2,1,0:T(2,128)}, f32[8,25,2,800]{3,2,1,0:T(2,128)}) custom-call(s32[2]{0:T(128)S(1)} %pad_add_fusion.refs_0_, s32[8]{0:T(128)S(1)} %copy-done.5, f32[8,2,8,800]{3,2,1,0:T(8,128)S(1)} %collective-permute-done.22.refs_2_, f32[8,2,8,800]{3,2,1,0:T(8,128)S(1)} %collective-permute-done.23.refs_3_, ...), custom_call_target="tpu_custom_call" | custom-call | tf_op jit(solution)/shard_map/pallas_call | solution.py:85
  128.6 8.8 %collective-permute-done.12.refs_3_ = f32[8,2432]{1,0:T(8,128)S(1)} collective-permute-done((f32[8,2432]{1,0:T(8,128)S(1)}, f32[8,2432]{1,0:T(8,128)S(1)}, u32[]{:S(2)}, u32[]{:S(2)}) %collective-permute-start.12) | collective-permute-done | bytes 77856 | tf_op jit(solution)/shard_map/ppermute | solution.py:313
  137.3 1.4 %shard_map.96 = f32[8,25,2,800]{3,2,1,0:T(2,128)} custom-call(s32[1]{0:T(128)} %bitcast.refs_0_, f32[8,2432]{1,0:T(8,128)S(1)} %copy-done.2, f32[8,2432]{1,0:T(8,128)S(1)} %collective-permute-done.11.refs_2_, f32[8,2432]{1,0:T(8,128)S(1)} %collective-permute-done.12.refs_3_, f32[8,2432]{1,0:T(8,128)S(1)} %collective-permute-done.13.refs_4_, ...), custom_call_target="tpu_custom_call" | custom-call | tf_op jit(solution)/shard_map/pallas_call | solution.py:85
  (58 shorter events, 9.1 us)
Async XLA Ops:
  3.4 6.0 %copy-start.7 = (f32[8,10112]{1,0:T(8,128)S(1)}, f32[8,10112]{1,0:T(8,128)}, u32[]{:S(2)}) copy-start(f32[8,10112]{1,0:T(8,128)} %get-tuple-element.51) | copy-start | bytes 970756
  3.4 8.6 %copy-start.6 = (f32[8,10112]{1,0:T(8,128)S(1)}, f32[8,10112]{1,0:T(8,128)}, u32[]{:S(2)}) copy-start(f32[8,10112]{1,0:T(8,128)} %get-tuple-element.52) | copy-start | bytes 970756
  5.5 12.8 %collective-permute-start.3 = (f32[4,2,8,800]{3,2,1,0:T(8,128)S(1)}, f32[4,2,8,800]{3,2,1,0:T(8,128)S(1)}, u32[]{:S(2)}, u32[]{:S(2)}) collective-permute-start(f32[4,2,8,800]{3,2,1,0:T(8,128)S(1)} %get-tuple-element.54), channel_id=1, source_target_pairs={{0,1},{2,3},{4,5},{6,7},{1,0},{3,2},{5,4},{7,6},{8,9},{10,11},{12,... | collective-permute-start | bytes 614408 | tf_op jit(solution)/shard_map/ppermute | solution.py:607
  6.0 12.2 %collective-permute-start.4 = (f32[4,2,8,800]{3,2,1,0:T(8,128)S(1)}, f32[4,2,8,800]{3,2,1,0:T(8,128)S(1)}, u32[]{:S(2)}, u32[]{:S(2)}) collective-permute-start(f32[4,2,8,800]{3,2,1,0:T(8,128)S(1)} %get-tuple-element.55), channel_id=1, source_target_pairs={{1,2},{3,4},{5,6},{2,1},{4,3},{6,5},{9,10},{11,12},{13,14},{10,9},... | collective-permute-start | bytes 614408 | tf_op jit(solution)/shard_map/ppermute | solution.py:607
  6.7 39.1 %collective-permute-start = (f32[8,10112]{1,0:T(8,128)S(1)}, f32[8,10112]{1,0:T(8,128)S(1)}, u32[]{:S(2)}, u32[]{:S(2)}) collective-permute-start(f32[8,10112]{1,0:T(8,128)S(1)} %copy-done.8), channel_id=1, source_target_pairs={{0,8},{8,16},{16,24},{24,0},{1,9},{9,17},{17,25},{25,1},{2,10},{10... | collective-permute-start | bytes 970760 | tf_op jit(solution)/shard_map/ppermute | solution.py:313
  9.4 36.5 %collective-permute-start.1 = (f32[8,10112]{1,0:T(8,128)S(1)}, f32[8,10112]{1,0:T(8,128)S(1)}, u32[]{:S(2)}, u32[]{:S(2)}) collective-permute-start(f32[8,10112]{1,0:T(8,128)S(1)} %copy-done.7), channel_id=1, source_target_pairs={{0,16},{8,24},{16,0},{24,8},{1,17},{9,25},{17,1},{25,9},{2,18},{10... | collective-permute-start | bytes 970760 | tf_op jit(solution)/shard_map/ppermute | solution.py:313
  12.0 35.9 %collective-permute-start.2 = (f32[8,10112]{1,0:T(8,128)S(1)}, f32[8,10112]{1,0:T(8,128)S(1)}, u32[]{:S(2)}, u32[]{:S(2)}) collective-permute-start(f32[8,10112]{1,0:T(8,128)S(1)} %copy-done.6), channel_id=1, source_target_pairs={{0,24},{8,0},{16,8},{24,16},{1,25},{9,1},{17,9},{25,17},{2,26},{10... | collective-permute-start | bytes 970760 | tf_op jit(solution)/shard_map/ppermute | solution.py:313
  22.5 27.3 %copy-start = (f32[8,10112]{1,0:T(8,128)S(1)}, f32[8,10112]{1,0:T(8,128)}, u32[]{:S(2)}) copy-start(f32[8,10112]{1,0:T(8,128)} %get-tuple-element.49.refs_1_.refs_2_) | copy-start | bytes 970756
  25.2 47.7 %copy-start.9 = (f32[8,7680]{1,0:T(8,128)S(1)}, f32[8,7680]{1,0:T(8,128)}, u32[]{:S(2)}) copy-start(f32[8,7680]{1,0:T(8,128)} %get-tuple-element.72) | copy-start | bytes 737284
  25.2 8.1 %collective-permute-start.8 = (f32[8,2432]{1,0:T(8,128)}, f32[8,2432]{1,0:T(8,128)S(1)}, u32[]{:S(2)}, u32[]{:S(2)}) collective-permute-start(f32[8,2432]{1,0:T(8,128)} %get-tuple-element.62), channel_id=1, source_target_pairs={{0,8},{8,16},{16,24},{24,0},{1,9},{9,17},{17,25},{25,1},{2,10},{10... | collective-permute-start | bytes 233480 | tf_op jit(solution)/shard_map/ppermute | solution.py:313
  26.0 46.2 %collective-permute-start.20 = (f32[4,2,8,800]{3,2,1,0:T(8,128)S(1)}, f32[4,2,8,800]{3,2,1,0:T(8,128)S(1)}, u32[]{:S(2)}, u32[]{:S(2)}) collective-permute-start(f32[4,2,8,800]{3,2,1,0:T(8,128)S(1)} %get-tuple-element.77), channel_id=1, source_target_pairs={{0,1},{2,3},{4,5},{6,7},{1,0},{3,2},{5,4},{7,6},{8,9},{10,11},{12,... | collective-permute-start | bytes 614408 | tf_op jit(solution)/shard_map/ppermute | solution.py:607
  33.3 11.8 %collective-permute-start.9 = (f32[8,2432]{1,0:T(8,128)}, f32[8,2432]{1,0:T(8,128)S(1)}, u32[]{:S(2)}, u32[]{:S(2)}) collective-permute-start(f32[8,2432]{1,0:T(8,128)} %get-tuple-element.63), channel_id=1, source_target_pairs={{0,16},{8,24},{16,0},{24,8},{1,17},{9,25},{17,1},{25,9},{2,18},{10... | collective-permute-start | bytes 233480 | tf_op jit(solution)/shard_map/ppermute | solution.py:313
  45.1 27.8 %collective-permute-start.21 = (f32[4,2,8,800]{3,2,1,0:T(8,128)S(1)}, f32[4,2,8,800]{3,2,1,0:T(8,128)S(1)}, u32[]{:S(2)}, u32[]{:S(2)}) collective-permute-start(f32[4,2,8,800]{3,2,1,0:T(8,128)S(1)} %get-tuple-element.78), channel_id=1, source_target_pairs={{1,2},{3,4},{5,6},{2,1},{4,3},{6,5},{9,10},{11,12},{13,14},{10,9},... | collective-permute-start | bytes 614408 | tf_op jit(solution)/shard_map/ppermute | solution.py:607
  45.8 5.3 %collective-permute-start.10 = (f32[8,2432]{1,0:T(8,128)}, f32[8,2432]{1,0:T(8,128)S(1)}, u32[]{:S(2)}, u32[]{:S(2)}) collective-permute-start(f32[8,2432]{1,0:T(8,128)} %get-tuple-element.64), channel_id=1, source_target_pairs={{0,24},{8,0},{16,8},{24,16},{1,25},{9,1},{17,9},{25,17},{2,26},{10... | collective-permute-start | bytes 233480 | tf_op jit(solution)/shard_map/ppermute | solution.py:313
  45.9 54.1 %collective-permute-start.14 = (f32[8,7680]{1,0:T(8,128)}, f32[8,7680]{1,0:T(8,128)S(1)}, u32[]{:S(2)}, u32[]{:S(2)}) collective-permute-start(f32[8,7680]{1,0:T(8,128)} %get-tuple-element.70), channel_id=1, source_target_pairs={{0,8},{8,16},{16,24},{24,0},{1,9},{9,17},{17,25},{25,1},{2,10},{10... | collective-permute-start | bytes 737288 | tf_op jit(solution)/shard_map/ppermute | solution.py:313
  47.9 52.5 %collective-permute-start.15 = (f32[8,7680]{1,0:T(8,128)}, f32[8,7680]{1,0:T(8,128)S(1)}, u32[]{:S(2)}, u32[]{:S(2)}) collective-permute-start(f32[8,7680]{1,0:T(8,128)} %get-tuple-element.71), channel_id=1, source_target_pairs={{0,16},{8,24},{16,0},{24,8},{1,17},{9,25},{17,1},{25,9},{2,18},{10... | collective-permute-start | bytes 737288 | tf_op jit(solution)/shard_map/ppermute | solution.py:313
  51.1 6.1 %collective-permute-start.5 = (f32[8,128]{1,0:T(8,128)S(1)}, f32[8,128]{1,0:T(8,128)S(1)}, u32[]{:S(2)}, u32[]{:S(2)}) collective-permute-start(f32[8,128]{1,0:T(8,128)S(1)} %shard_map.89.refs_0_), channel_id=1, source_target_pairs={{0,8},{8,16},{16,24},{24,0},{1,9},{9,17},{17,25},{25,1},{2,10},{10... | collective-permute-start | bytes 12296 | tf_op jit(solution)/shard_map/ppermute | solution.py:313
  57.2 9.4 %collective-permute-start.6 = (f32[8,128]{1,0:T(8,128)S(1)}, f32[8,128]{1,0:T(8,128)S(1)}, u32[]{:S(2)}, u32[]{:S(2)}) collective-permute-start(f32[8,128]{1,0:T(8,128)S(1)} %shard_map.89.refs_0_), channel_id=1, source_target_pairs={{0,16},{8,24},{16,0},{24,8},{1,17},{9,25},{17,1},{25,9},{2,18},{10... | collective-permute-start | bytes 12296 | tf_op jit(solution)/shard_map/ppermute | solution.py:313
  66.6 3.6 %collective-permute-start.7 = (f32[8,128]{1,0:T(8,128)S(1)}, f32[8,128]{1,0:T(8,128)S(1)}, u32[]{:S(2)}, u32[]{:S(2)}) collective-permute-start(f32[8,128]{1,0:T(8,128)S(1)} %shard_map.89.refs_0_), channel_id=1, source_target_pairs={{0,24},{8,0},{16,8},{24,16},{1,25},{9,1},{17,9},{25,17},{2,26},{10... | collective-permute-start | bytes 12296 | tf_op jit(solution)/shard_map/ppermute | solution.py:313
  70.3 38.7 %collective-permute-start.24 = (f32[8,2,8,800]{3,2,1,0:T(8,128)S(1)}, f32[8,2,8,800]{3,2,1,0:T(8,128)S(1)}, u32[]{:S(2)}, u32[]{:S(2)}) collective-permute-start(f32[8,2,8,800]{3,2,1,0:T(8,128)S(1)} %get-tuple-element.82), channel_id=1, source_target_pairs={{0,1},{2,3},{4,5},{6,7},{1,0},{3,2},{5,4},{7,6},{8,9},{10,11},{12,... | collective-permute-start | bytes 1228808 | tf_op jit(solution)/shard_map/ppermute | solution.py:607
  72.2 37.8 %collective-permute-start.25 = (f32[8,2,8,800]{3,2,1,0:T(8,128)S(1)}, f32[8,2,8,800]{3,2,1,0:T(8,128)S(1)}, u32[]{:S(2)}, u32[]{:S(2)}) collective-permute-start(f32[8,2,8,800]{3,2,1,0:T(8,128)S(1)} %get-tuple-element.83), channel_id=1, source_target_pairs={{1,2},{3,4},{5,6},{2,1},{4,3},{6,5},{9,10},{11,12},{13,14},{10,9},... | collective-permute-start | bytes 1228808 | tf_op jit(solution)/shard_map/ppermute | solution.py:607
  72.9 29.5 %collective-permute-start.16 = (f32[8,7680]{1,0:T(8,128)S(1)}, f32[8,7680]{1,0:T(8,128)S(1)}, u32[]{:S(2)}, u32[]{:S(2)}) collective-permute-start(f32[8,7680]{1,0:T(8,128)S(1)} %copy-done.9), channel_id=1, source_target_pairs={{0,24},{8,0},{16,8},{24,16},{1,25},{9,1},{17,9},{25,17},{2,26},{10... | collective-permute-start | bytes 737288 | tf_op jit(solution)/shard_map/ppermute | solution.py:313
  100.0 12.9 %collective-permute-start.22 = (f32[8,2,8,800]{3,2,1,0:T(8,128)S(1)}, f32[8,2,8,800]{3,2,1,0:T(8,128)S(1)}, u32[]{:S(2)}, u32[]{:S(2)}) collective-permute-start(f32[8,2,8,800]{3,2,1,0:T(8,128)S(1)} %get-tuple-element.79), channel_id=1, source_target_pairs={{0,1},{2,3},{4,5},{6,7},{1,0},{3,2},{5,4},{7,6},{8,9},{10,11},{12,... | collective-permute-start | bytes 1228808 | tf_op jit(solution)/shard_map/ppermute | solution.py:607
  100.4 14.3 %collective-permute-start.23 = (f32[8,2,8,800]{3,2,1,0:T(8,128)S(1)}, f32[8,2,8,800]{3,2,1,0:T(8,128)S(1)}, u32[]{:S(2)}, u32[]{:S(2)}) collective-permute-start(f32[8,2,8,800]{3,2,1,0:T(8,128)S(1)} %get-tuple-element.80), channel_id=1, source_target_pairs={{1,2},{3,4},{5,6},{2,1},{4,3},{6,5},{9,10},{11,12},{13,14},{10,9},... | collective-permute-start | bytes 1228808 | tf_op jit(solution)/shard_map/ppermute | solution.py:607
  102.4 6.4 %collective-permute-start.11 = (f32[8,2432]{1,0:T(8,128)}, f32[8,2432]{1,0:T(8,128)S(1)}, u32[]{:S(2)}, u32[]{:S(2)}) collective-permute-start(f32[8,2432]{1,0:T(8,128)} %get-tuple-element.66), channel_id=1, source_target_pairs={{0,8},{8,16},{16,24},{24,0},{1,9},{9,17},{17,25},{25,1},{2,10},{10... | collective-permute-start | bytes 233480 | tf_op jit(solution)/shard_map/ppermute | solution.py:313
  104.6 8.4 %copy-start.11 = (f32[8,2432]{1,0:T(8,128)S(1)}, f32[8,2432]{1,0:T(8,128)}, u32[]{:S(2)}) copy-start(f32[8,2432]{1,0:T(8,128)} %get-tuple-element.67) | copy-start | bytes 233476
  104.6 10.1 %copy-start.10 = (f32[8,2432]{1,0:T(8,128)S(1)}, f32[8,2432]{1,0:T(8,128)}, u32[]{:S(2)}) copy-start(f32[8,2432]{1,0:T(8,128)} %get-tuple-element.68) | copy-start | bytes 233476
  108.8 28.5 %collective-permute-start.17 = (f32[8,7680]{1,0:T(8,128)}, f32[8,7680]{1,0:T(8,128)S(1)}, u32[]{:S(2)}, u32[]{:S(2)}) collective-permute-start(f32[8,7680]{1,0:T(8,128)} %get-tuple-element.74), channel_id=1, source_target_pairs={{0,8},{8,16},{16,24},{24,0},{1,9},{9,17},{17,25},{25,1},{2,10},{10... | collective-permute-start | bytes 737288 | tf_op jit(solution)/shard_map/ppermute | solution.py:313
  109.0 28.3 %collective-permute-start.18 = (f32[8,7680]{1,0:T(8,128)}, f32[8,7680]{1,0:T(8,128)S(1)}, u32[]{:S(2)}, u32[]{:S(2)}) collective-permute-start(f32[8,7680]{1,0:T(8,128)} %get-tuple-element.75), channel_id=1, source_target_pairs={{0,16},{8,24},{16,0},{24,8},{1,17},{9,25},{17,1},{25,9},{2,18},{10... | collective-permute-start | bytes 737288 | tf_op jit(solution)/shard_map/ppermute | solution.py:313
  110.0 27.3 %collective-permute-start.19 = (f32[8,7680]{1,0:T(8,128)}, f32[8,7680]{1,0:T(8,128)S(1)}, u32[]{:S(2)}, u32[]{:S(2)}) collective-permute-start(f32[8,7680]{1,0:T(8,128)} %get-tuple-element.76), channel_id=1, source_target_pairs={{0,24},{8,0},{16,8},{24,16},{1,25},{9,1},{17,9},{25,17},{2,26},{10... | collective-permute-start | bytes 737288 | tf_op jit(solution)/shard_map/ppermute | solution.py:313
  112.9 24.4 %collective-permute-start.12 = (f32[8,2432]{1,0:T(8,128)S(1)}, f32[8,2432]{1,0:T(8,128)S(1)}, u32[]{:S(2)}, u32[]{:S(2)}) collective-permute-start(f32[8,2432]{1,0:T(8,128)S(1)} %copy-done.11), channel_id=1, source_target_pairs={{0,16},{8,24},{16,0},{24,8},{1,17},{9,25},{17,1},{25,9},{2,18},{10... | collective-permute-start | bytes 233480 | tf_op jit(solution)/shard_map/ppermute | solution.py:313
  114.7 22.6 %collective-permute-start.13 = (f32[8,2432]{1,0:T(8,128)S(1)}, f32[8,2432]{1,0:T(8,128)S(1)}, u32[]{:S(2)}, u32[]{:S(2)}) collective-permute-start(f32[8,2432]{1,0:T(8,128)S(1)} %copy-done.10), channel_id=1, source_target_pairs={{0,24},{8,0},{16,8},{24,16},{1,25},{9,1},{17,9},{25,17},{2,26},{10... | collective-permute-start | bytes 233480 | tf_op jit(solution)/shard_map/ppermute | solution.py:313
  (6 other events, 19.2 us)

commit v2 on v1

--- a/solution.py
+++ b/solution.py
@@ -368,7 +368,7 @@
     )
 
 
-def medium_body(side_ref, cells_ref, ghosts_ref, prev_ref, coef_ref, still_ref, out_ref, inner_ref, outer_ref, arrive, leave):
+def medium_body(cells_ref, ghosts_ref, prev_ref, coef_ref, still_ref, out_ref, arrive, leave):
     own, width, depth, across = cells_ref.shape
 
     def one(x, carry):
@@ -392,21 +392,17 @@
     for k, (low, high) in enumerate(blocks_of(width)):
         arrive(k)
         lax.fori_loop(low, high, one, 0)
-    for k, ref in enumerate((coef_ref, still_ref)):
-        rows = slice(k * GHOST, (k + 1) * GHOST)
-        edges_of(side_ref, ref, inner_ref.at[rows], outer_ref.at[rows])
-
-
-def medium(side, cells, ghosts, prev, after=()):
+
+
+def medium(cells, ghosts, prev, after=()):
     own, width, depth, across = cells.shape
-    edge = held((2 * GHOST, depth, own, across))
     return call(
         medium_body,
-        out_shape=[held((width, depth, own, across))] * 3 + [edge] * 2,
-        in_specs=[SMEM] + [VMEM] * 3,
-        out_specs=[VMEM] * 5,
-        operands=[side, cells, ghosts, prev],
-        near=(1, 2, 3),
+        out_shape=[held((width, depth, own, across))] * 3,
+        in_specs=[VMEM] * 3,
+        out_specs=[VMEM] * 3,
+        operands=[cells, ghosts, prev],
+        near=(0, 1, 2),
         after=after,
     )
 
@@ -440,20 +436,20 @@
                 near, slope = up + down, up - down
                 even = (0.5 * (weights[2] + weights[4])) * near + weights[3] * row[t]
                 odd = (0.5 * (weights[2] - weights[4])) * slope
-                sums[0, x, z, :, tile(t)] = weights[1] * near + (3.0 * weights[0]) * row[t]
-                sums[1, x, z, :, tile(t)] = even - odd
-                sums[2, x, z, :, tile(t)] = even + odd
+                sums[0, x & 1, z, :, tile(t)] = weights[1] * near + (3.0 * weights[0]) * row[t]
+                sums[1, x & 1, z, :, tile(t)] = even - odd
+                sums[2, x & 1, z, :, tile(t)] = even + odd
 
     def advance(x):
         for z in range(depth):
-            plus = [sums[1, x, z, :, tile(t)] for t in range(tiles)]
-            minus = [sums[2, x, z, :, tile(t)] for t in range(tiles)]
+            plus = [sums[1, x & 1, z, :, tile(t)] for t in range(tiles)]
+            minus = [sums[2, x & 1, z, :, tile(t)] for t in range(tiles)]
             for t in range(tiles):
                 count = min(LANES, across - t * LANES)
                 if count <= 0:
                     continue
                 here = tile(t)
-                total = sums[0, x, z, :, here]
+                total = sums[0, x & 1, z, :, here]
                 for offset in range(1, GHOST + 1):
                     pair = wide[x + GHOST + offset, z, :, here] + wide[x + GHOST - offset, z, :, here]
                     if z - offset >= 0:
@@ -482,7 +478,7 @@
 
 
 def wave_body(
-    amplitude, side_ref, source_ref, inner_ref, outer_ref, now_ref, prev_ref, coef_ref, still_ref,
+    amplitude, reach, side_ref, source_ref, inner_ref, outer_ref, now_ref, prev_ref, coef_ref, still_ref,
     out_ref, to_inner_ref, to_outer_ref, wide, sums,
 ):
     width, _, _, across = now_ref.shape
@@ -490,9 +486,13 @@
     def store(x, z, there, value):
         out_ref[x, z, :, there] = value
 
-    between(side_ref, wide, inner_ref, now_ref, outer_ref)
+    between(side_ref, wide, inner_ref.at[0:GHOST], now_ref, outer_ref.at[0:GHOST])
     sweep(amplitude, across, width, 0, side_ref, source_ref, wide, sums, prev_ref, coef_ref, still_ref, store)
-    edges_of(side_ref, out_ref, to_inner_ref, to_outer_ref)
+    low = 0
+    for count, ref in zip(reach, (out_ref, coef_ref, still_ref)):
+        rows = slice(low, low + count)
+        edges_of(side_ref, ref, to_inner_ref.at[rows], to_outer_ref.at[rows])
+        low += count
 
 
 def lanes_of(across):
@@ -503,14 +503,14 @@
     width, depth, own, across = now.shape
     lanes = lanes_of(across)
     return call(
-        functools.partial(wave_body, amplitude),
-        out_shape=[held(now.shape)] + [held((reach,) + now.shape[1:])] * 2,
+        functools.partial(wave_body, amplitude, reach),
+        out_shape=[held(now.shape)] + [held((sum(reach),) + now.shape[1:])] * 2,
         in_specs=[SMEM] * 2 + [VMEM] * 6,
         out_specs=[VMEM] * 3,
         operands=[side, source, *edges, now, prev, coef, still],
         scratch_shapes=[
             pltpu.VMEM((width + 2 * GHOST, depth, own, lanes), jnp.float32),
-            pltpu.VMEM((3, width, depth, own, lanes), jnp.float32),
+            pltpu.VMEM((3, 2, depth, own, lanes), jnp.float32),
         ],
         after=after,
     )
@@ -518,7 +518,7 @@
 
 def last_body(
     amplitudes, side_ref, source_ref, inner_ref, outer_ref, now_ref, before_inner, before_outer, prev_ref,
-    medium_inner, medium_outer, coef_ref, still_ref, token_ref, first_ref, second_ref,
+    coef_ref, still_ref, token_ref, first_ref, second_ref,
     wide, middle, prev, coef, still, sums,
 ):
     width, depth, own, across = now_ref.shape
@@ -526,10 +526,9 @@
     start = (across // LANES) * LANES
     token_ref[...] = jnp.zeros(token_ref.shape, jnp.float32)
     between(side_ref, wide, inner_ref, now_ref, outer_ref)
-    between(side_ref, prev, before_inner, prev_ref, before_outer)
-    halves = [slice(0, GHOST), slice(GHOST, 2 * GHOST)]
-    between(side_ref, coef, medium_inner.at[halves[0]], coef_ref, medium_outer.at[halves[0]])
-    between(side_ref, still, medium_inner.at[halves[1]], still_ref, medium_outer.at[halves[1]])
+    for k, (part, ref) in enumerate(((prev, prev_ref), (coef, coef_ref), (still, still_ref))):
+        rows = slice(k * GHOST, (k + 1) * GHOST)
+        between(side_ref, part, before_inner.at[rows], ref, before_outer.at[rows])
 
     def clear(x, carry):
         for z in range(depth):
@@ -557,7 +556,7 @@
     sweep(amplitudes[1], across, width, 0, side_ref, source_ref, middle, sums, own_rows, coef_ref, still_ref, store)
 
 
-def last_steps(amplitudes, side, source, edges, now, before, prev, around, coef, still, after=()):
+def last_steps(amplitudes, side, source, edges, now, before, prev, coef, still, after=()):
     width, depth, own, across = now.shape
     lanes = lanes_of(across)
     extended = pltpu.VMEM((width + 2 * GHOST, depth, own, lanes), jnp.float32)
@@ -565,16 +564,16 @@
     return call(
         functools.partial(last_body, amplitudes),
         out_shape=[held((own, LANES)), native, native],
-        in_specs=[SMEM] * 2 + [VMEM] * 10,
+        in_specs=[SMEM] * 2 + [VMEM] * 8,
         out_specs=[VMEM] * 3,
-        operands=[side, source, *edges, now, *before, prev, *around, coef, still],
+        operands=[side, source, *edges, now, *before, prev, coef, still],
         scratch_shapes=[
             pltpu.VMEM((width + 4 * GHOST, depth, own, lanes), jnp.float32),
             extended,
             extended,
             extended,
             extended,
-            pltpu.VMEM((3, width + 2 * GHOST, depth, own, lanes), jnp.float32),
+            pltpu.VMEM((3, 2, depth, own, lanes), jnp.float32),
         ],
         after=after,
     )
@@ -600,7 +599,7 @@
 
     side = jnp.stack([space_idx % 2, space_idx * width]).astype(jnp.int32)
     now, inner, outer = hold(side, turned(wave_now))
-    coef, still, prev, *around = medium(side, turned(particles), turned(ghosts), turned(wave_prev), after=[now])
+    coef, still, prev = medium(turned(particles), turned(ghosts), turned(wave_prev), after=[now])
 
     def swap(edge, first):
         pairs = [(i, i + 1) for i in range(first, spaces - 1, 2)]
@@ -612,10 +611,9 @@
     amplitudes = [2.0 * math.cos(1.3 * index) for index in range(STEPS)]
     waves = [prev, now]
     edges = swapped(inner, outer)
-    around = swapped(*around)
 
     def step(index, edges, after=()):
-        reach = GHOST if index < STEPS - 3 else 2 * GHOST
+        reach = (2 * GHOST,) if index == STEPS - 3 else (GHOST,) * (3 if index == STEPS - 4 else 1)
         out, inner, outer = wave_step(
             amplitudes[index], reach, side, src_cell, edges, waves[-1], waves[-2], coef, still, after=after
         )
@@ -641,7 +639,7 @@
         order = out[0]
         moved += exchange(out, members)
     token, *ends = last_steps(
-        amplitudes[-2:], side, src_cell, edges, waves[-1], before, waves[-2], around, coef, still, after=[order]
+        amplitudes[-2:], side, src_cell, edges, waves[-1], before, waves[-2], coef, still, after=[order]
     )
     new_particles = unpacked(pack, cuts, me, moved, after=[token])[0]
     return turned(new_particles), turned(ends[0]), turned(ends[1])

time: 141 us -> 123 us (0.87)
  blocking collectives: 20.6 us -> 11.2 us
  waiting for transfers between devices: 34.1 us -> 27.6 us
    all_gather x1, blocking collectives: 20.6 us -> 11.2 us  [shards(): dist = lax.all_gather(dist, 'space', axis=0)]
    ppermute x18, waiting for transfers between devices: 34.1 us -> 27.5 us  [exchange(): lax.ppermute(parts[shift], 'member', [(i, (i + shift) % members) for i in...]
    ppermute x8 -> x6, starting transfers between devices: 7.32 us -> 7.75 us  [swap(): return lax.ppermute(edge, 'space', pairs + [(j, i) for i, j in pairs])]
  transfers between devices with their start and end apart: 26 -> 24, of which waited for: 7 -> 4; matrix products, arithmetic and copies ran while one was open for 0% -> 0% of each run, Pallas kernels for 24% -> 23%
where the time goes in v2:
time: 123 us; the launch traced here: 122 us
  starting transfers between devices  41.6 us (34%)
  Pallas kernels  38.5 us (31%)
  waiting for transfers between devices  27.6 us (22%)
  blocking collectives  11.2 us (9%)
  local copies, waits for them, and re-layouts  1.89 us (2%)
    pallas_call x12, Pallas kernels, call(): pl.pallas_call(ordered, out_shape=out_shape, in_specs=in_specs + [ANY] *...  38.5 us
    ppermute x18, starting transfers between devices, exchange(): lax.ppermute(parts[shift], 'member', [(i, (i + shift) % members) for i in...  33.8 us
    ppermute x18, waiting for transfers between devices, exchange(): lax.ppermute(parts[shift], 'member', [(i, (i + shift) % members) for i in...  27.5 us
    all_gather x1, blocking collectives, shards(): dist = lax.all_gather(dist, 'space', axis=0)  11.2 us
    ppermute x6, starting transfers between devices, swap(): return lax.ppermute(edge, 'space', pairs + [(j, i) for i, j in pairs])  7.75 us
  transfers between devices with their start and end apart: 24, of which 4 were waited for; matrix products, arithmetic and copies ran while one was open for 0% of the time, Pallas kernels for 23%

profile of v2, /device:TPU:0, one launch (start us, length us, event | category | flops | bytes accessed | tf_op | source)
XLA Modules:
  0.0 121.7 jit_solution(141973715325025452)
XLA Ops:
  0.6 2.7 %shard_map.85 = (f32[8,10112]{1,0:T(8,128)}, f32[8,10112]{1,0:T(8,128)}, f32[8,10112]{1,0:T(8,128)}, f32[8,10112]{1,0:T(8,128)}) custom-call(s32[1]{0:T(128)} %bitcast.refs_0_, f32[8,25,2,800]{3,2,1,0:T(2,128)} %bitcast.17), custom_call_target="tpu_custom_call" | custom-call | tf_op jit(solution)/shard_map/pallas_call | solution.py:85
  3.4 2.0 %shard_map.86 = (f32[25,2,8,800]{3,2,1,0:T(8,128)S(1)}, f32[4,2,8,800]{3,2,1,0:T(8,128)S(1)}, f32[4,2,8,800]{3,2,1,0:T(8,128)S(1)}) custom-call(s32[2]{0:T(128)S(1)} %pad_add_fusion.refs_0_, f32[8,25,2,800]{3,2,1,0:T(2,128)} %bitcast.19), custom_call_target="tpu_custom_call" | custom-call | tf_op jit(solution)/shard_map/pallas_call | solution.py:85
  6.7 4.3 %shard_map.87 = (f32[25,2,8,800]{3,2,1,0:T(8,128)S(1)}, f32[25,2,8,800]{3,2,1,0:T(8,128)S(1)}, f32[25,2,8,800]{3,2,1,0:T(8,128)S(1)}) custom-call(f32[8,25,2,800]{3,2,1,0:T(2,128)} %bitcast.18, f32[8,25,8,800]{3,2,1,0:T(8,128)} %bitcast.16, f32[8,25,2,800]{3,2,1,0:T(2,128)} %bitcast.22, f32[25,2,8,800]{3,2,1,0:T(8,128)S(1)} %get-tuple-element.54.refs_3_.refs_4_.refs_5_), custom_call_target="tpu_custom_call" | custom-call | tf_op jit(solution)/shard_map/pallas_call | solution.py:85
  11.1 4.3 %shard_map.88 = (f32[25,2,8,800]{3,2,1,0:T(8,128)S(1)}, f32[12,2,8,800]{3,2,1,0:T(8,128)S(1)}, f32[12,2,8,800]{3,2,1,0:T(8,128)S(1)}) custom-call(s32[2]{0:T(128)S(1)} %pad_add_fusion.refs_0_, s32[8]{0:T(128)S(1)} %copy-done.5, f32[4,2,8,800]{3,2,1,0:T(8,128)S(1)} %collective-permute-done.3.refs_2_, f32[4,2,8,800]{3,2,1,0:T(8,128)S(1)} %collective-permute-done.4.refs_3_, ...), custom_call_target="tpu_custom_call" | custom-call | tf_op jit(solution)/shard_map/pallas_call | solution.py:85
  15.4 4.8 %collective-permute-start.20 = (f32[12,2,8,800]{3,2,1,0:T(8,128)S(1)}, f32[12,2,8,800]{3,2,1,0:T(8,128)S(1)}, u32[]{:S(2)}, u32[]{:S(2)}) collective-permute-start(f32[12,2,8,800]{3,2,1,0:T(8,128)S(1)} %get-tuple-element.75), channel_id=1, source_target_pairs={{0,1},{2,3},{4,5},{6,7},{1,0},{3,2},{5,4},{7,6},{8,9},{10,11},{12,... | collective-permute-start | bytes 1843208 | tf_op jit(solution)/shard_map/ppermute | solution.py:606
  20.2 0.7 collective-permute-start.21
  20.9 2.9 %collective-permute-start = (f32[8,10112]{1,0:T(8,128)S(1)}, f32[8,10112]{1,0:T(8,128)S(1)}, u32[]{:S(2)}, u32[]{:S(2)}) collective-permute-start(f32[8,10112]{1,0:T(8,128)S(1)} %copy-done.8), channel_id=1, source_target_pairs={{0,8},{8,16},{16,24},{24,0},{1,9},{9,17},{17,25},{25,1},{2,10},{10... | collective-permute-start | bytes 970760 | tf_op jit(solution)/shard_map/ppermute | solution.py:313
  23.8 2.6 %collective-permute-start.1 = (f32[8,10112]{1,0:T(8,128)S(1)}, f32[8,10112]{1,0:T(8,128)S(1)}, u32[]{:S(2)}, u32[]{:S(2)}) collective-permute-start(f32[8,10112]{1,0:T(8,128)S(1)} %copy-done.7), channel_id=1, source_target_pairs={{0,16},{8,24},{16,0},{24,8},{1,17},{9,25},{17,1},{25,9},{2,18},{10... | collective-permute-start | bytes 970760 | tf_op jit(solution)/shard_map/ppermute | solution.py:313
  26.4 1.3 %collective-permute-start.2 = (f32[8,10112]{1,0:T(8,128)S(1)}, f32[8,10112]{1,0:T(8,128)S(1)}, u32[]{:S(2)}, u32[]{:S(2)}) collective-permute-start(f32[8,10112]{1,0:T(8,128)S(1)} %copy-done.6), channel_id=1, source_target_pairs={{0,24},{8,0},{16,8},{24,16},{1,25},{9,1},{17,9},{25,17},{2,26},{10... | collective-permute-start | bytes 970760 | tf_op jit(solution)/shard_map/ppermute | solution.py:313
  27.7 2.7 %shard_map.91 = (f32[8,2432]{1,0:T(8,128)}, f32[8,2432]{1,0:T(8,128)}, f32[8,2432]{1,0:T(8,128)}, f32[8,2432]{1,0:T(8,128)}, f32[8,7680]{1,0:T(8,128)}, /*index=...) custom-call(s32[1]{0:T(128)} %bitcast.refs_0_, f32[8,25,2,800]{3,2,1,0:T(2,128)} %bitcast.20, ...), custom_call_target="tpu_custom_call" | custom-call | tf_op jit(solution)/shard_map/pallas_call | solution.py:85
  30.4 1.3 %collective-permute-done.refs_2_.refs_3_ = f32[8,10112]{1,0:T(8,128)S(1)} collective-permute-done((f32[8,10112]{1,0:T(8,128)S(1)}, f32[8,10112]{1,0:T(8,128)S(1)}, u32[]{:S(2)}, u32[]{:S(2)}) %collective-permute-start) | collective-permute-done | bytes 323616 | tf_op jit(solution)/shard_map/ppermute | solution.py:313
  31.8 17.1 %collective-permute-done.1.refs_3_.refs_4_ = f32[8,10112]{1,0:T(8,128)S(1)} collective-permute-done((f32[8,10112]{1,0:T(8,128)S(1)}, f32[8,10112]{1,0:T(8,128)S(1)}, u32[]{:S(2)}, u32[]{:S(2)}) %collective-permute-start.1) | collective-permute-done | bytes 323616 | tf_op jit(solution)/shard_map/ppermute | solution.py:313
  48.9 1.3 %shard_map.89.refs_0_ = f32[8,128]{1,0:T(8,128)S(1)} custom-call(s32[1]{0:T(128)} %bitcast.refs_0_, f32[8,10112]{1,0:T(8,128)S(1)} %copy-done, f32[8,10112]{1,0:T(8,128)S(1)} %collective-permute-done.refs_2_.refs_3_, f32[8,10112]{1,0:T(8,128)S(1)} %collective-permute-done.1.refs_3_.refs_4_, f32[8,10112]{1,0:T(8,128)S(1)} %collective-permute-done.2.refs_4_.refs_5_, ...), custom_call_target="tpu_custom_call" | custom-call | tf_op jit(solution)/shard_map/pallas_call | solution.py:85
  50.2 8.3 %collective-permute-start.5 = (f32[8,128]{1,0:T(8,128)S(1)}, f32[8,128]{1,0:T(8,128)S(1)}, u32[]{:S(2)}, u32[]{:S(2)}) collective-permute-start(f32[8,128]{1,0:T(8,128)S(1)} %shard_map.89.refs_0_), channel_id=1, source_target_pairs={{0,8},{8,16},{16,24},{24,0},{1,9},{9,17},{17,25},{25,1},{2,10},{10... | collective-permute-start | bytes 12296 | tf_op jit(solution)/shard_map/ppermute | solution.py:313
  58.6 2.4 %collective-permute-start.7 = (f32[8,128]{1,0:T(8,128)S(1)}, f32[8,128]{1,0:T(8,128)S(1)}, u32[]{:S(2)}, u32[]{:S(2)}) collective-permute-start(f32[8,128]{1,0:T(8,128)S(1)} %shard_map.89.refs_0_), channel_id=1, source_target_pairs={{0,24},{8,0},{16,8},{24,16},{1,25},{9,1},{17,9},{25,17},{2,26},{10... | collective-permute-start | bytes 12296 | tf_op jit(solution)/shard_map/ppermute | solution.py:313
  61.0 1.2 collective-permute-start.14
  62.2 0.9 collective-permute-done.6.refs_2_
  63.5 2.9 %collective-permute-start.10 = (f32[8,2432]{1,0:T(8,128)S(1)}, f32[8,2432]{1,0:T(8,128)S(1)}, u32[]{:S(2)}, u32[]{:S(2)}) collective-permute-start(f32[8,2432]{1,0:T(8,128)S(1)} %copy-done.12), channel_id=1, source_target_pairs={{0,24},{8,0},{16,8},{24,16},{1,25},{9,1},{17,9},{25,17},{2,26},{10... | collective-permute-start | bytes 233480 | tf_op jit(solution)/shard_map/ppermute | solution.py:313
  67.0 1.1 collective-permute-start.16
  68.0 11.2 %all-gather = f32[64,128]{1,0:T(8,128)S(1)} all-gather(f32[8,128]{1,0:T(8,128)S(1)} %shard_map.90), channel_id=2, replica_groups=mesh['member'=4,'space'=8] {'space'}, dimensions={0}, use_global_device_ids=true | all-gather | bytes 36864 | tf_op jit(solution)/shard_map/all_gather | solution.py:631
  79.2 4.3 %shard_map.94 = (f32[25,2,8,800]{3,2,1,0:T(8,128)S(1)}, f32[8,2,8,800]{3,2,1,0:T(8,128)S(1)}, f32[8,2,8,800]{3,2,1,0:T(8,128)S(1)}) custom-call(s32[2]{0:T(128)S(1)} %pad_add_fusion.refs_0_, s32[8]{0:T(128)S(1)} %copy-done.5, f32[12,2,8,800]{3,2,1,0:T(8,128)S(1)} %collective-permute-done.20.refs_2_.refs_5_, ...), custom_call_target="tpu_custom_call" | custom-call | tf_op jit(solution)/shard_map/pallas_call | solution.py:85
  84.7 1.3 %shard_map.92 = (f32[8,2432]{1,0:T(8,128)}, f32[8,2432]{1,0:T(8,128)}, f32[8,2432]{1,0:T(8,128)}, f32[8,2432]{1,0:T(8,128)}) custom-call(s32[1]{0:T(128)} %bitcast.refs_0_, f32[8,8,128]{2,1,0:T(8,128)S(1)} %bitcast.13, f32[8,10112]{1,0:T(8,128)S(1)} %copy-done, f32[8,10112]{1,0:T(8,128)S(1)} %collective-permute-done.refs_2_.refs_3_, ...), custom_call_target="tpu_custom_call" | custom-call | tf_op jit(solution)/shard_map/pallas_call | solution.py:85
  86.0 1.0 collective-permute-start.11
  87.0 0.9 copy-done.2
  87.8 2.2 %shard_map.93 = (f32[8,7680]{1,0:T(8,128)}, f32[8,7680]{1,0:T(8,128)}, f32[8,7680]{1,0:T(8,128)}, f32[8,7680]{1,0:T(8,128)}) custom-call(s32[1]{0:T(128)} %bitcast.refs_0_, f32[8,8,128]{2,1,0:T(8,128)S(1)} %bitcast.15, f32[8,10112]{1,0:T(8,128)S(1)} %copy-done, f32[8,10112]{1,0:T(8,128)S(1)} %collective-permute-done.refs_2_.refs_3_, ...), custom_call_target="tpu_custom_call" | custom-call | tf_op jit(solution)/shard_map/pallas_call | solution.py:85
  90.0 4.7 %collective-permute-start.17 = (f32[8,7680]{1,0:T(8,128)}, f32[8,7680]{1,0:T(8,128)S(1)}, u32[]{:S(2)}, u32[]{:S(2)}) collective-permute-start(f32[8,7680]{1,0:T(8,128)} %get-tuple-element.72), channel_id=1, source_target_pairs={{0,8},{8,16},{16,24},{24,0},{1,9},{9,17},{17,25},{25,1},{2,10},{10... | collective-permute-start | bytes 737288 | tf_op jit(solution)/shard_map/ppermute | solution.py:313
  94.7 2.4 %collective-permute-start.19 = (f32[8,7680]{1,0:T(8,128)}, f32[8,7680]{1,0:T(8,128)S(1)}, u32[]{:S(2)}, u32[]{:S(2)}) collective-permute-start(f32[8,7680]{1,0:T(8,128)} %get-tuple-element.74), channel_id=1, source_target_pairs={{0,24},{8,0},{16,8},{24,16},{1,25},{9,1},{17,9},{25,17},{2,26},{10... | collective-permute-start | bytes 737288 | tf_op jit(solution)/shard_map/ppermute | solution.py:313
  97.7 1.5 %collective-permute-start.13 = (f32[8,2432]{1,0:T(8,128)S(1)}, f32[8,2432]{1,0:T(8,128)S(1)}, u32[]{:S(2)}, u32[]{:S(2)}) collective-permute-start(f32[8,2432]{1,0:T(8,128)S(1)} %copy-done.14), channel_id=1, source_target_pairs={{0,24},{8,0},{16,8},{24,16},{1,25},{9,1},{17,9},{25,17},{2,26},{10... | collective-permute-start | bytes 233480 | tf_op jit(solution)/shard_map/ppermute | solution.py:313
  99.2 0.9 copy-done.1
  100.1 11.9 %shard_map.95 = (f32[8,128]{1,0:T(8,128)S(1)}, f32[8,25,2,800]{3,2,1,0:T(2,128)}, f32[8,25,2,800]{3,2,1,0:T(2,128)}) custom-call(s32[2]{0:T(128)S(1)} %pad_add_fusion.refs_0_, s32[8]{0:T(128)S(1)} %copy-done.5, f32[8,2,8,800]{3,2,1,0:T(8,128)S(1)} %collective-permute-done.22.refs_2_, f32[8,2,8,800]{3,2,1,0:T(8,128)S(1)} %collective-permute-done.23.refs_3_, ...), custom_call_target="tpu_custom_call" | custom-call | tf_op jit(solution)/shard_map/pallas_call | solution.py:85
  112.0 8.2 %collective-permute-done.12.refs_3_ = f32[8,2432]{1,0:T(8,128)S(1)} collective-permute-done((f32[8,2432]{1,0:T(8,128)S(1)}, f32[8,2432]{1,0:T(8,128)S(1)}, u32[]{:S(2)}, u32[]{:S(2)}) %collective-permute-start.12) | collective-permute-done | bytes 77856 | tf_op jit(solution)/shard_map/ppermute | solution.py:313
  120.3 1.4 %shard_map.96 = f32[8,25,2,800]{3,2,1,0:T(2,128)} custom-call(s32[1]{0:T(128)} %bitcast.refs_0_, f32[8,2432]{1,0:T(8,128)S(1)} %copy-done.2, f32[8,2432]{1,0:T(8,128)S(1)} %collective-permute-done.11.refs_2_, f32[8,2432]{1,0:T(8,128)S(1)} %collective-permute-done.12.refs_3_, f32[8,2432]{1,0:T(8,128)S(1)} %collective-permute-done.13.refs_4_, ...), custom_call_target="tpu_custom_call" | custom-call | tf_op jit(solution)/shard_map/pallas_call | solution.py:85
  (62 shorter events, 4.1 us)
Async XLA Ops:
  5.4 5.6 %collective-permute-start.3 = (f32[4,2,8,800]{3,2,1,0:T(8,128)S(1)}, f32[4,2,8,800]{3,2,1,0:T(8,128)S(1)}, u32[]{:S(2)}, u32[]{:S(2)}) collective-permute-start(f32[4,2,8,800]{3,2,1,0:T(8,128)S(1)} %get-tuple-element.52), channel_id=1, source_target_pairs={{0,1},{2,3},{4,5},{6,7},{1,0},{3,2},{5,4},{7,6},{8,9},{10,11},{12,... | collective-permute-start | bytes 614408 | tf_op jit(solution)/shard_map/ppermute | solution.py:606
  6.0 5.0 %collective-permute-start.4 = (f32[4,2,8,800]{3,2,1,0:T(8,128)S(1)}, f32[4,2,8,800]{3,2,1,0:T(8,128)S(1)}, u32[]{:S(2)}, u32[]{:S(2)}) collective-permute-start(f32[4,2,8,800]{3,2,1,0:T(8,128)S(1)} %get-tuple-element.53), channel_id=1, source_target_pairs={{1,2},{3,4},{5,6},{2,1},{4,3},{6,5},{9,10},{11,12},{13,14},{10,9},... | collective-permute-start | bytes 614408 | tf_op jit(solution)/shard_map/ppermute | solution.py:606
  11.1 12.7 %copy-start.7 = (f32[8,10112]{1,0:T(8,128)S(1)}, f32[8,10112]{1,0:T(8,128)}, u32[]{:S(2)}) copy-start(f32[8,10112]{1,0:T(8,128)} %get-tuple-element.49) | copy-start | bytes 970756
  11.1 15.3 %copy-start.6 = (f32[8,10112]{1,0:T(8,128)S(1)}, f32[8,10112]{1,0:T(8,128)}, u32[]{:S(2)}) copy-start(f32[8,10112]{1,0:T(8,128)} %get-tuple-element.50) | copy-start | bytes 970756
  15.4 51.0 %collective-permute-start.20 = (f32[12,2,8,800]{3,2,1,0:T(8,128)S(1)}, f32[12,2,8,800]{3,2,1,0:T(8,128)S(1)}, u32[]{:S(2)}, u32[]{:S(2)}) collective-permute-start(f32[12,2,8,800]{3,2,1,0:T(8,128)S(1)} %get-tuple-element.75), channel_id=1, source_target_pairs={{0,1},{2,3},{4,5},{6,7},{1,0},{3,2},{5,4},{7,6},{8,9},{10,11},{12,... | collective-permute-start | bytes 1843208 | tf_op jit(solution)/shard_map/ppermute | solution.py:606
  20.2 46.8 %collective-permute-start.21 = (f32[12,2,8,800]{3,2,1,0:T(8,128)S(1)}, f32[12,2,8,800]{3,2,1,0:T(8,128)S(1)}, u32[]{:S(2)}, u32[]{:S(2)}) collective-permute-start(f32[12,2,8,800]{3,2,1,0:T(8,128)S(1)} %get-tuple-element.76), channel_id=1, source_target_pairs={{1,2},{3,4},{5,6},{2,1},{4,3},{6,5},{9,10},{11,12},{13,14},{10,9},... | collective-permute-start | bytes 1843208 | tf_op jit(solution)/shard_map/ppermute | solution.py:606
  20.9 10.9 %collective-permute-start = (f32[8,10112]{1,0:T(8,128)S(1)}, f32[8,10112]{1,0:T(8,128)S(1)}, u32[]{:S(2)}, u32[]{:S(2)}) collective-permute-start(f32[8,10112]{1,0:T(8,128)S(1)} %copy-done.8), channel_id=1, source_target_pairs={{0,8},{8,16},{16,24},{24,0},{1,9},{9,17},{17,25},{25,1},{2,10},{10... | collective-permute-start | bytes 970760 | tf_op jit(solution)/shard_map/ppermute | solution.py:313
  23.8 25.1 %collective-permute-start.1 = (f32[8,10112]{1,0:T(8,128)S(1)}, f32[8,10112]{1,0:T(8,128)S(1)}, u32[]{:S(2)}, u32[]{:S(2)}) collective-permute-start(f32[8,10112]{1,0:T(8,128)S(1)} %copy-done.7), channel_id=1, source_target_pairs={{0,16},{8,24},{16,0},{24,8},{1,17},{9,25},{17,1},{25,9},{2,18},{10... | collective-permute-start | bytes 970760 | tf_op jit(solution)/shard_map/ppermute | solution.py:313
  26.4 22.5 %collective-permute-start.2 = (f32[8,10112]{1,0:T(8,128)S(1)}, f32[8,10112]{1,0:T(8,128)S(1)}, u32[]{:S(2)}, u32[]{:S(2)}) collective-permute-start(f32[8,10112]{1,0:T(8,128)S(1)} %copy-done.6), channel_id=1, source_target_pairs={{0,24},{8,0},{16,8},{24,16},{1,25},{9,1},{17,9},{25,17},{2,26},{10... | collective-permute-start | bytes 970760 | tf_op jit(solution)/shard_map/ppermute | solution.py:313
  27.7 21.2 %copy-start = (f32[8,10112]{1,0:T(8,128)S(1)}, f32[8,10112]{1,0:T(8,128)}, u32[]{:S(2)}) copy-start(f32[8,10112]{1,0:T(8,128)} %get-tuple-element.47.refs_1_.refs_2_) | copy-start | bytes 970756
  30.4 30.6 %copy-start.11 = (f32[8,7680]{1,0:T(8,128)S(1)}, f32[8,7680]{1,0:T(8,128)}, u32[]{:S(2)}) copy-start(f32[8,7680]{1,0:T(8,128)} %get-tuple-element.68) | copy-start | bytes 737284
  30.4 32.7 %copy-start.13 = (f32[8,2432]{1,0:T(8,128)S(1)}, f32[8,2432]{1,0:T(8,128)}, u32[]{:S(2)}) copy-start(f32[8,2432]{1,0:T(8,128)} %get-tuple-element.61) | copy-start | bytes 233476
  30.4 33.1 %copy-start.12 = (f32[8,2432]{1,0:T(8,128)S(1)}, f32[8,2432]{1,0:T(8,128)}, u32[]{:S(2)}) copy-start(f32[8,2432]{1,0:T(8,128)} %get-tuple-element.62) | copy-start | bytes 233476
  30.4 36.0 %copy-start.10 = (f32[8,7680]{1,0:T(8,128)S(1)}, f32[8,7680]{1,0:T(8,128)}, u32[]{:S(2)}) copy-start(f32[8,7680]{1,0:T(8,128)} %get-tuple-element.69) | copy-start | bytes 737284
  30.4 36.5 %copy-start.9 = (f32[8,7680]{1,0:T(8,128)S(1)}, f32[8,7680]{1,0:T(8,128)}, u32[]{:S(2)}) copy-start(f32[8,7680]{1,0:T(8,128)} %get-tuple-element.70) | copy-start | bytes 737284
  31.8 26.8 %collective-permute-start.8 = (f32[8,2432]{1,0:T(8,128)}, f32[8,2432]{1,0:T(8,128)S(1)}, u32[]{:S(2)}, u32[]{:S(2)}) collective-permute-start(f32[8,2432]{1,0:T(8,128)} %get-tuple-element.60), channel_id=1, source_target_pairs={{0,8},{8,16},{16,24},{24,0},{1,9},{9,17},{17,25},{25,1},{2,10},{10... | collective-permute-start | bytes 233480 | tf_op jit(solution)/shard_map/ppermute | solution.py:313
  50.2 10.8 %collective-permute-start.5 = (f32[8,128]{1,0:T(8,128)S(1)}, f32[8,128]{1,0:T(8,128)S(1)}, u32[]{:S(2)}, u32[]{:S(2)}) collective-permute-start(f32[8,128]{1,0:T(8,128)S(1)} %shard_map.89.refs_0_), channel_id=1, source_target_pairs={{0,8},{8,16},{16,24},{24,0},{1,9},{9,17},{17,25},{25,1},{2,10},{10... | collective-permute-start | bytes 12296 | tf_op jit(solution)/shard_map/ppermute | solution.py:313
  58.6 4.5 %collective-permute-start.6 = (f32[8,128]{1,0:T(8,128)S(1)}, f32[8,128]{1,0:T(8,128)S(1)}, u32[]{:S(2)}, u32[]{:S(2)}) collective-permute-start(f32[8,128]{1,0:T(8,128)S(1)} %shard_map.89.refs_0_), channel_id=1, source_target_pairs={{0,16},{8,24},{16,0},{24,8},{1,17},{9,25},{17,1},{25,9},{2,18},{10... | collective-permute-start | bytes 12296 | tf_op jit(solution)/shard_map/ppermute | solution.py:313
  58.6 5.0 %collective-permute-start.7 = (f32[8,128]{1,0:T(8,128)S(1)}, f32[8,128]{1,0:T(8,128)S(1)}, u32[]{:S(2)}, u32[]{:S(2)}) collective-permute-start(f32[8,128]{1,0:T(8,128)S(1)} %shard_map.89.refs_0_), channel_id=1, source_target_pairs={{0,24},{8,0},{16,8},{24,16},{1,25},{9,1},{17,9},{25,17},{2,26},{10... | collective-permute-start | bytes 12296 | tf_op jit(solution)/shard_map/ppermute | solution.py:313
  61.0 25.0 %collective-permute-start.14 = (f32[8,7680]{1,0:T(8,128)S(1)}, f32[8,7680]{1,0:T(8,128)S(1)}, u32[]{:S(2)}, u32[]{:S(2)}) collective-permute-start(f32[8,7680]{1,0:T(8,128)S(1)} %copy-done.11), channel_id=1, source_target_pairs={{0,8},{8,16},{16,24},{24,0},{1,9},{9,17},{17,25},{25,1},{2,10},{10... | collective-permute-start | bytes 737288 | tf_op jit(solution)/shard_map/ppermute | solution.py:313
  63.1 20.5 %collective-permute-start.9 = (f32[8,2432]{1,0:T(8,128)S(1)}, f32[8,2432]{1,0:T(8,128)S(1)}, u32[]{:S(2)}, u32[]{:S(2)}) collective-permute-start(f32[8,2432]{1,0:T(8,128)S(1)} %copy-done.13), channel_id=1, source_target_pairs={{0,16},{8,24},{16,0},{24,8},{1,17},{9,25},{17,1},{25,9},{2,18},{10... | collective-permute-start | bytes 233480 | tf_op jit(solution)/shard_map/ppermute | solution.py:313
  63.5 20.4 %collective-permute-start.10 = (f32[8,2432]{1,0:T(8,128)S(1)}, f32[8,2432]{1,0:T(8,128)S(1)}, u32[]{:S(2)}, u32[]{:S(2)}) collective-permute-start(f32[8,2432]{1,0:T(8,128)S(1)} %copy-done.12), channel_id=1, source_target_pairs={{0,24},{8,0},{16,8},{24,16},{1,25},{9,1},{17,9},{25,17},{2,26},{10... | collective-permute-start | bytes 233480 | tf_op jit(solution)/shard_map/ppermute | solution.py:313
  66.5 20.5 %collective-permute-start.15 = (f32[8,7680]{1,0:T(8,128)S(1)}, f32[8,7680]{1,0:T(8,128)S(1)}, u32[]{:S(2)}, u32[]{:S(2)}) collective-permute-start(f32[8,7680]{1,0:T(8,128)S(1)} %copy-done.10), channel_id=1, source_target_pairs={{0,16},{8,24},{16,0},{24,8},{1,17},{9,25},{17,1},{25,9},{2,18},{10... | collective-permute-start | bytes 737288 | tf_op jit(solution)/shard_map/ppermute | solution.py:313
  67.0 20.0 %collective-permute-start.16 = (f32[8,7680]{1,0:T(8,128)S(1)}, f32[8,7680]{1,0:T(8,128)S(1)}, u32[]{:S(2)}, u32[]{:S(2)}) collective-permute-start(f32[8,7680]{1,0:T(8,128)S(1)} %copy-done.9), channel_id=1, source_target_pairs={{0,24},{8,0},{16,8},{24,16},{1,25},{9,1},{17,9},{25,17},{2,26},{10... | collective-permute-start | bytes 737288 | tf_op jit(solution)/shard_map/ppermute | solution.py:313
  83.6 13.5 %collective-permute-start.22 = (f32[8,2,8,800]{3,2,1,0:T(8,128)S(1)}, f32[8,2,8,800]{3,2,1,0:T(8,128)S(1)}, u32[]{:S(2)}, u32[]{:S(2)}) collective-permute-start(f32[8,2,8,800]{3,2,1,0:T(8,128)S(1)} %get-tuple-element.77), channel_id=1, source_target_pairs={{0,1},{2,3},{4,5},{6,7},{1,0},{3,2},{5,4},{7,6},{8,9},{10,11},{12,... | collective-permute-start | bytes 1228808 | tf_op jit(solution)/shard_map/ppermute | solution.py:606
  84.0 13.7 %collective-permute-start.23 = (f32[8,2,8,800]{3,2,1,0:T(8,128)S(1)}, f32[8,2,8,800]{3,2,1,0:T(8,128)S(1)}, u32[]{:S(2)}, u32[]{:S(2)}) collective-permute-start(f32[8,2,8,800]{3,2,1,0:T(8,128)S(1)} %get-tuple-element.78), channel_id=1, source_target_pairs={{1,2},{3,4},{5,6},{2,1},{4,3},{6,5},{9,10},{11,12},{13,14},{10,9},... | collective-permute-start | bytes 1228808 | tf_op jit(solution)/shard_map/ppermute | solution.py:606
  86.0 8.7 %collective-permute-start.11 = (f32[8,2432]{1,0:T(8,128)}, f32[8,2432]{1,0:T(8,128)S(1)}, u32[]{:S(2)}, u32[]{:S(2)}) collective-permute-start(f32[8,2432]{1,0:T(8,128)} %get-tuple-element.64), channel_id=1, source_target_pairs={{0,8},{8,16},{16,24},{24,0},{1,9},{9,17},{17,25},{25,1},{2,10},{10... | collective-permute-start | bytes 233480 | tf_op jit(solution)/shard_map/ppermute | solution.py:313
  90.0 30.3 %collective-permute-start.17 = (f32[8,7680]{1,0:T(8,128)}, f32[8,7680]{1,0:T(8,128)S(1)}, u32[]{:S(2)}, u32[]{:S(2)}) collective-permute-start(f32[8,7680]{1,0:T(8,128)} %get-tuple-element.72), channel_id=1, source_target_pairs={{0,8},{8,16},{16,24},{24,0},{1,9},{9,17},{17,25},{25,1},{2,10},{10... | collective-permute-start | bytes 737288 | tf_op jit(solution)/shard_map/ppermute | solution.py:313
  94.7 25.6 %collective-permute-start.18 = (f32[8,7680]{1,0:T(8,128)}, f32[8,7680]{1,0:T(8,128)S(1)}, u32[]{:S(2)}, u32[]{:S(2)}) collective-permute-start(f32[8,7680]{1,0:T(8,128)} %get-tuple-element.73), channel_id=1, source_target_pairs={{0,16},{8,24},{16,0},{24,8},{1,17},{9,25},{17,1},{25,9},{2,18},{10... | collective-permute-start | bytes 737288 | tf_op jit(solution)/shard_map/ppermute | solution.py:313
  94.7 25.6 %collective-permute-start.19 = (f32[8,7680]{1,0:T(8,128)}, f32[8,7680]{1,0:T(8,128)S(1)}, u32[]{:S(2)}, u32[]{:S(2)}) collective-permute-start(f32[8,7680]{1,0:T(8,128)} %get-tuple-element.74), channel_id=1, source_target_pairs={{0,24},{8,0},{16,8},{24,16},{1,25},{9,1},{17,9},{25,17},{2,26},{10... | collective-permute-start | bytes 737288 | tf_op jit(solution)/shard_map/ppermute | solution.py:313
  97.1 23.2 %collective-permute-start.12 = (f32[8,2432]{1,0:T(8,128)S(1)}, f32[8,2432]{1,0:T(8,128)S(1)}, u32[]{:S(2)}, u32[]{:S(2)}) collective-permute-start(f32[8,2432]{1,0:T(8,128)S(1)} %copy-done.15), channel_id=1, source_target_pairs={{0,16},{8,24},{16,0},{24,8},{1,17},{9,25},{17,1},{25,9},{2,18},{10... | collective-permute-start | bytes 233480 | tf_op jit(solution)/shard_map/ppermute | solution.py:313
  97.7 22.5 %collective-permute-start.13 = (f32[8,2432]{1,0:T(8,128)S(1)}, f32[8,2432]{1,0:T(8,128)S(1)}, u32[]{:S(2)}, u32[]{:S(2)}) collective-permute-start(f32[8,2432]{1,0:T(8,128)S(1)} %copy-done.14), channel_id=1, source_target_pairs={{0,24},{8,0},{16,8},{24,16},{1,25},{9,1},{17,9},{25,17},{2,26},{10... | collective-permute-start | bytes 233480 | tf_op jit(solution)/shard_map/ppermute | solution.py:313
  (8 other events, 44.0 us)
